TPU v7x, 32 devices: a whole 2x2x4 slice. The times are simulated.
32 devices in a mesh: dp: 16 (over z, y, core), mp: 2 (over x).
Axes of the slice: x: 2, y: 2, z: 4, core: 2. Of those that a mesh axis runs over, the one named last changes fastest.
Arguments:
- tokens: bfloat16 [32768, 768], P('dp'), may hold values from -6 to 6
- grad_out: bfloat16 [32768, 768], P('dp'), may hold values from -6 to 6
- head_perm: int32 [32, 12], P('dp', 'mp'), may hold values from 0 to 1
- block_mask: int32 [32, 12, 3], P('dp', 'mp'), may hold values 0 or 1
- w_qkv: bfloat16 [768, 3, 768], P('dp', None, 'mp'), may hold values from -0.3125 to 0.3125
- b_qv: bfloat16 [2, 768], P(None, ('mp', 'dp')), may hold values from -3 to 3
- w_out: bfloat16 [768, 768], P('mp', 'dp'), may hold values from -0.625 to 0.625
- b_out: bfloat16 [768], P('dp'), may hold values from -3 to 3
- gain_one: bfloat16 [768], P('dp'), may hold values from 0.25 to 1.75
- shift_one: bfloat16 [768], P('dp'), may hold values from -2 to 2
- w_up: bfloat16 [768, 3072], P('dp', 'mp'), may hold values from -0.21875 to 0.21875
- b_up: bfloat16 [3072], P(('mp', 'dp')), may hold values from -3 to 3
- w_down: bfloat16 [3072, 768], P('mp', 'dp'), may hold values from -0.15625 to 0.15625
- b_down: bfloat16 [768], P('dp'), may hold values from -2 to 2
- gain_two: bfloat16 [768], P('dp'), may hold values from 0.25 to 1.75
- shift_two: bfloat16 [768], P('dp'), may hold values from -2 to 2
Outputs:
- output: bfloat16 [32768, 768], P('dp')
- input_grad: float32 [32768, 768], P('dp')
- grad_w_qkv: float32 [768, 3, 768], P('dp', None, 'mp')
- grad_b_qv: float32 [2, 768], P(None, ('mp', 'dp'))
- grad_w_out: float32 [768, 768], P('mp', 'dp')
- grad_b_out: float32 [768], P('dp')
- grad_gain_one: float32 [768], P('dp')
- grad_shift_one: float32 [768], P('dp')
- grad_w_up: float32 [768, 3072], P('dp', 'mp')
- grad_b_up: float32 [3072], P(('mp', 'dp'))
- grad_w_down: float32 [3072, 768], P('mp', 'dp')
- grad_b_down: float32 [768], P('dp')
- grad_gain_two: float32 [768], P('dp')
- grad_shift_two: float32 [768], P('dp')
Inputs may be any that keep to these rules, and one draw needn't show every extreme that they name: `head_perm`: 0 pairs each half with itself, 1 pairs it with the other half. `block_mask`: entry a + b is the keep flag of block a of the queries with block b of the keys (b <= a).
All inputs are finite; a program needn't handle non-finite values.
Results may differ from a plain program's by a relative error of at most 0.015.
The roundings to bfloat16 on the way count: a program that leaves them out, or rounds other values in their place, can miss the bound.
Values may be sent and summed in bfloat16 or wider, within the bound.
No kernel may reach another device: no remote copies, remote signals or barrier semaphores. Data moves between devices by JAX's collectives and lax.ppermute only.
A program may use at most 256 MiB of HBM per device.

v0:
```python
import functools

import jax
import jax.numpy as jnp
from jax import lax
from jax.experimental import pallas as pl
from jax.experimental.pallas import tpu as pltpu
from jax.sharding import PartitionSpec as P

HD = 64
PAIR = 2 * HD
BLOCK = 256
HALF = 2 * BLOCK
NORM_EPS = 1e-05
BF = jnp.bfloat16
F32 = jnp.float32
AXES = ("dp", "mp")
NN = (((1,), (0,)), ((), ()))
NT = (((1,), (1,)), ((), ()))
TN = (((0,), (0,)), ((), ()))
SMALL = 128


def mm(first, second, dims):
    return lax.dot_general(first, second, dims, preferred_element_type=F32)


def cost(microseconds):
    return pl.CostEstimate(
        flops=int(microseconds * 4 * 1e9),
        transcendentals=0,
        bytes_accessed=int(microseconds * 4 * 3e6),
    )


def pairs_of(step):
    moves = []
    for d in range(16):
        for m in range(2):
            d2, m2 = step(d, m)
            moves.append((2 * d + m, 2 * d2 + m2))
    return moves


MOVE_X = pairs_of(lambda d, m: (d, 1 - m))
MOVE_Y = pairs_of(lambda d, m: (d ^ 2, m))
MOVE_CORE = pairs_of(lambda d, m: (d ^ 1, m))
MOVE_Z = [pairs_of(lambda d, m, k=k: ((d + 4 * k) % 16, m)) for k in (1, 2, 3)]
MOVE_FIRST = pairs_of(lambda d, m: (d ^ 2, m) if d & 1 else (d, 1 - m))
MOVE_SECOND = pairs_of(lambda d, m: (d, 1 - m) if d & 1 else (d ^ 2, m))


MOVE_REDUCE = MOVE_SECOND, MOVE_FIRST


def move(values, moves):
    return lax.ppermute(values, AXES, moves)


def swap_mp(values):
    return lax.ppermute(values, "mp", [(0, 1), (1, 0)])


def started(copies):
    for copy in copies:
        copy.start()
    return copies


def piece_copies(where, pieces, target, sem, by_core=False):
    if len(pieces[0].shape) == 4:
        (whole,) = pieces
        count, _, rows, _ = whole.shape
        return started(
            [
                pltpu.make_async_copy(
                    whole.at[d, where[3] ^ half],
                    target.at[half, pl.ds(d * rows, rows), :],
                    sem.at[(half * count + d) // 4, d % 4],
                )
                for half in range(2)
                for d in range(count)
            ]
        )
    if len(pieces[0].shape) == 2:
        return started(
            [pltpu.make_async_copy(p, target.at[n], sem.at[n, 0]) for n, p in enumerate(pieces)]
        )
    rows = pieces[0].shape[1]
    z, y, core = where[0], where[1], where[2]

    def copies(ref, half, dy, dcore, slot):
        out = []
        for k in range(4):
            block = ((lax.rem(z + 4 - k, 4) * 2 + (y ^ dy)) * 2 + (core ^ dcore)) * rows
            block = pl.multiple_of(block, 16)
            out.append(
                pltpu.make_async_copy(
                    ref.at[k], target.at[half, pl.ds(block, rows), :], sem.at[slot, k]
                )
            )
        return out

    waits = []
    if not by_core:
        for slot, ref in enumerate(pieces):
            waits += copies(ref, slot // 4, slot % 2, slot % 4 // 2, slot)
        return started(waits)

    z0, a0, b0, c0, z1, a1, b1, c1 = pieces
    first = core == 0
    for slot, (ref, half, dy, dcore) in enumerate(
        ((z0, 0, 0, 0), (c0, 1, 1, 0), (z1, 0, 0, 1), (c1, 1, 1, 1))
    ):
        waits += copies(ref, half, dy, dcore, slot)
    started(waits)
    for slot, (ref_if, ref_else, half, dy, dcore) in enumerate(
        ((b0, a0, 0, 1, 0), (a0, b0, 1, 0, 0), (a1, b1, 0, 1, 1), (b1, a1, 1, 0, 1)), 4
    ):
        @pl.when(first)
        def _(ref=ref_if, half=half, dy=dy, dcore=dcore, slot=slot):
            started(copies(ref, half, dy, dcore, slot))

        @pl.when(jnp.logical_not(first))
        def _(ref=ref_else, half=half, dy=dy, dcore=dcore, slot=slot):
            started(copies(ref, half, dy, dcore, slot))

        waits += copies(ref_if, half, dy, dcore, slot)
    return waits


def device_of(rows, half, d_model):
    row = lax.broadcasted_iota(jnp.int32, (d_model, 1), 0)
    device = lax.div(row, jnp.int32(rows))
    return device, row - device * rows


def one_hot(target, cols):
    lane = lax.broadcasted_iota(jnp.int32, (target.shape[0], cols), 1)
    return jnp.where(lane == target, 1.0, 0.0).astype(BF)


def qv_places(rows, d_model):
    device, at = device_of(rows, rows // 2, d_model)
    value = (at >= rows // 2).astype(jnp.int32)
    target = value * (d_model // 2) + device * (rows // 2) + at - value * (rows // 2)
    return one_hot(target, d_model)


def up_places(rows, d_model, part, ff):
    device, at = device_of(rows, rows, d_model)
    return one_hot(device * (2 * rows) + part * rows + at, ff)


def project_kernel(rows, n_qkv, where, tok_ref, *refs):
    pieces = refs[:n_qkv]
    proj_ref, vec_ref, up_ref, weights, bias, sem = refs[n_qkv:]
    d_model = tok_ref.shape[1]
    span = proj_ref.shape[1]

    @pl.when(pl.program_id(0) == 0)
    def _():
        for copy in piece_copies(where, pieces, weights, sem):
            copy.wait()
        bias[...] = jnp.zeros_like(bias)
        qv = qv_places(rows, d_model)
        up = [up_places(rows, d_model, part, up_ref.shape[1]) for part in range(2)]
        turned = weights[0, :, span:].T[:16]
        vec_ref[...] = turned[:8].astype(F32)
        row = mm(turned, qv, NN)[8:9]
        for pair in range(span // (3 * PAIR)):
            at = pair * 3 * PAIR
            bias[0:1, at : at + PAIR] = row[:, pair * PAIR : (pair + 1) * PAIR]
            first = d_model // 2 + pair * PAIR
            bias[0:1, at + 2 * PAIR : at + 3 * PAIR] = row[:, first : first + PAIR]
        up_ref[...] = mm(turned, up[0], NN)[6:7] + mm(turned, up[1], NN)[7:8]

    tokens = tok_ref[...]
    for at in range(0, span, 384):
        proj_ref[:, at : at + 384] = (
            mm(tokens, weights[0, :, at : at + 384], NN) + bias[0:1, at : at + 384]
        ).astype(BF)


def project(where, tokens, pieces, rows, seq, span, ff, tile=512):
    d_model = tokens.shape[1]
    return pl.pallas_call(
        functools.partial(project_kernel, rows, len(pieces)),
        out_shape=(
            jax.ShapeDtypeStruct((seq, span), BF),
            jax.ShapeDtypeStruct((8, d_model), F32),
            jax.ShapeDtypeStruct((1, ff), F32),
        ),
        grid_spec=pltpu.PrefetchScalarGridSpec(
            num_scalar_prefetch=1,
            grid=(seq // tile,),
            in_specs=[own_tile(tile, d_model, seq)] + [ANYWHERE] * len(pieces),
            out_specs=[
                row_tile(tile, span),
                pl.BlockSpec((8, d_model), lambda i, w: (0, 0)),
                pl.BlockSpec((1, ff), lambda i, w: (0, 0)),
            ],
            scratch_shapes=[
                pltpu.VMEM((1, d_model, span + SMALL), BF),
                pltpu.VMEM((8, span), F32),
                pltpu.SemaphoreType.DMA((8, 4)),
            ],
        ),
        cost_estimate=cost(8.7),
        name="project",
    )(where, tokens, *pieces)


def last_kernel(n_qkv, where, own_ref, other_ref, one_ref, *refs):
    pieces = refs[:n_qkv]
    whole_ref, low_ref, weights, sem = refs[n_qkv:]
    span = own_ref.shape[1]

    @pl.when(pl.program_id(0) == 0)
    def _():
        for copy in piece_copies(where, pieces, weights, sem):
            copy.wait()

    total = (
        mm(own_ref[...], weights[0, :, :span], NT)
        + mm(other_ref[...], weights[1, :, :span], NT)
        + one_ref[...]
    )
    whole_ref[...] = total
    low_ref[...] = total.astype(BF)


def last_part(where, d_proj, d_one, pieces, tile=512):
    seq, span = d_proj[0].shape
    d_model = d_one.shape[1]
    return pl.pallas_call(
        functools.partial(last_kernel, len(pieces)),
        out_shape=(
            jax.ShapeDtypeStruct((2 * seq, d_model), F32),
            jax.ShapeDtypeStruct((seq, d_model), BF),
        ),
        grid_spec=pltpu.PrefetchScalarGridSpec(
            num_scalar_prefetch=1,
            grid=(seq // tile,),
            in_specs=[row_tile(tile, span), row_tile(tile, span), row_tile(tile, d_model)]
            + [ANYWHERE] * len(pieces),
            out_specs=[own_tile(tile, d_model, seq), row_tile(tile, d_model)],
            scratch_shapes=[
                pltpu.VMEM((2, d_model, span + SMALL), BF),
                pltpu.SemaphoreType.DMA((8, 4)),
            ],
        ),
        cost_estimate=cost(12.0),
        name="last_part",
    )(where, *d_proj, d_one, *pieces)


def part_copies(where, result, half, keep_ref, send_ref, sem, staged):
    if not staged:
        return [pltpu.make_async_copy(result.at[half], keep_ref.at[half], sem.at[half, 0])]
    if len(keep_ref.shape) == 4:
        rows = keep_ref.shape[2]
        return [
            pltpu.make_async_copy(
                result.at[half, pl.ds(d * rows, rows), :],
                keep_ref.at[d, where[3] ^ half],
                sem.at[half, d],
            )
            for d in range(keep_ref.shape[0])
        ]
    rows = keep_ref.shape[-2]
    z, y, core = where[0], where[1], where[2]
    out = []
    for dcore, target in enumerate((keep_ref, send_ref)):
        for dy in range(2):
            for k in range(4):
                block = ((lax.rem(z + k, 4) * 2 + (y ^ dy)) * 2 + (core ^ dcore)) * rows
                block = pl.multiple_of(block, 16)
                if target.shape[2] == 1:
                    place = target.at[dy, k, 0]
                else:
                    by_y = (core ^ dcore) == 0
                    place = target.at[jnp.where(by_y, dy, half), jnp.where(by_y, half, dy), k]
                out.append(
                    pltpu.make_async_copy(
                        result.at[half, pl.ds(block, rows), :], place, sem.at[half, len(out)]
                    )
                )
    return out


def part_shapes(staged, halves, d_model, cols):
    if not staged:
        whole = jax.ShapeDtypeStruct((halves, d_model, cols), BF)
        return whole, jax.ShapeDtypeStruct((8, 128), BF)
    rows = d_model // 16
    dims = (2, 4, 1, rows, cols) if halves == 1 else (2, 2, 4, rows, cols)
    return (jax.ShapeDtypeStruct(dims, BF),) * 2


def after(value, *others):
    return lax.optimization_barrier((value, *others))[0]


def grads_kernel(staged, rows, halves, widths, n_extra, where, *refs):
    count = len(widths)
    lhs_refs, refs = refs[:count], refs[count:]
    rhs_refs, refs = refs[: count * halves], refs[count * halves :]
    extra_refs, refs = refs[:n_extra], refs[n_extra:]
    keep_ref, send_ref, result, turned, sem = refs
    d_model = result.shape[1]
    for lhs, out in zip(lhs_refs, range(count)):
        for at in range(0, lhs.shape[0], BLOCK):
            turned[out, :, at : at + BLOCK] = lhs[at : at + BLOCK, :].T
    for half in range(halves):
        first = 0
        for n in range(count):
            rhs = rhs_refs[n * halves + half]
            rhs = rhs.at[half] if len(rhs.shape) == 3 else rhs
            width = rhs.shape[1]
            for at in range(0, width, 384):
                result[half, :, first + at : first + at + 384] = mm(
                    turned[n], rhs[:, at : at + 384], NN
                ).astype(BF)
            first += width
        if n_extra == 1:
            (sums,) = extra_refs
            blank = jnp.zeros((SMALL - 1, PAIR), F32)
            parts = [
                sums[pair, 0:1, n * PAIR : (n + 1) * PAIR]
                for n in (0, 2)
                for pair in range(sums.shape[0])
            ]
            line = jnp.concatenate(parts, axis=1)
            lines = jnp.concatenate([line, jnp.zeros((SMALL - 1, line.shape[1]), F32)], axis=0)
            extra = mm(qv_places(rows, d_model), lines.astype(BF), NT)
        else:
            two, one, up = extra_refs
            own = one_hot(lax.broadcasted_iota(jnp.int32, (d_model, 1), 0), d_model)
            zero = jnp.zeros((SMALL - 6, d_model), F32)
            lines = jnp.concatenate([one[2:3], one[0:2], two[2:3], two[0:2], zero], axis=0)
            extra = mm(own, lines.astype(BF), NT)
            blank = jnp.zeros((SMALL - 8, up.shape[2]), F32)
            for part in range(2):
                line = up[half, 0:1]
                before = jnp.zeros((6 + part, line.shape[1]), F32)
                behind = jnp.zeros((SMALL - 7 - part, line.shape[1]), F32)
                lines = jnp.concatenate([before, line, behind], axis=0)
                extra = extra + mm(
                    up_places(rows, d_model, part, line.shape[1]), lines.astype(BF), NT
                )
        result[half, :, first:] = extra.astype(BF)
        for copy in part_copies(where, result, half, keep_ref, send_ref, sem, staged):
            copy.start()
    for half in range(halves):
        for copy in part_copies(where, result, half, keep_ref, send_ref, sem, staged):
            copy.wait()


def whole_spec(array):
    return pl.BlockSpec(array.shape, lambda i, w, n=array.ndim: (0,) * n)


def own_tile(tile, width, seq):
    return pl.BlockSpec((tile, width), lambda i, w: (w[3] * (seq // tile) + i, 0))


def grads(where, staged, rows, lhs, rhs, extra):
    halves = len(rhs[0])
    seq = rhs[0][0].shape[-2]
    d_model = lhs[0].shape[1]
    widths = [r[0].shape[-1] for r in rhs]
    cols = sum(widths) + SMALL
    operands = [*(r for pair in rhs for r in pair), *extra]
    return pl.pallas_call(
        functools.partial(grads_kernel, staged, rows, halves, widths, len(extra)),
        out_shape=part_shapes(staged, halves, d_model, cols),
        grid_spec=pltpu.PrefetchScalarGridSpec(
            num_scalar_prefetch=1,
            grid=(1,),
            in_specs=[
                own_tile(seq, d_model, seq) if l.shape[0] > seq else whole_spec(l) for l in lhs
            ]
            + [whole_spec(o) for o in operands],
            out_specs=[ANYWHERE] * 2,
            scratch_shapes=[
                pltpu.VMEM((halves, d_model, cols), BF),
                pltpu.VMEM((len(lhs), d_model, seq), BF),
                pltpu.SemaphoreType.DMA((halves, 16)),
            ],
        ),
        cost_estimate=cost(20.0 if halves == 2 else 7.2),
        name="grads",
    )(where, *lhs, *operands)


def row_norm(values):
    centered = values - jnp.mean(values, axis=-1, keepdims=True)
    inverse = lax.rsqrt(jnp.mean(centered * centered, axis=-1, keepdims=True) + NORM_EPS)
    return centered * inverse, inverse


def row_norm_back(d_normed, z, inverse, gain):
    dz = d_normed * gain
    return (
        dz - jnp.mean(dz, axis=-1, keepdims=True) - z * jnp.mean(dz * z, axis=-1, keepdims=True)
    ) * inverse


def column_sum(values):
    return jnp.sum(values, axis=0, keepdims=True)


def first_kernel(n_up, where, tok_ref, ctx0_ref, ctx1_ref, vec_ref, bias0_ref, bias1_ref, *refs):
    pieces = refs[:n_up]
    z_ref, inv_ref, hid_ref, slope_ref, weights, sem = refs[n_up:]
    bias_refs = bias0_ref, bias1_ref
    width = ctx0_ref.shape[1]

    @pl.when(pl.program_id(0) == 0)
    def _():
        for copy in piece_copies(where, pieces, weights, sem, True):
            copy.wait()

    resid = (
        tok_ref[...].astype(F32)
        + mm(ctx0_ref[...], weights[0, :, :width], NT)
        + mm(ctx1_ref[...], weights[1, :, :width], NT)
        + vec_ref[0:1]
    )
    z, inverse = row_norm(resid)
    z_ref[...] = z
    inv_ref[...] = jnp.broadcast_to(inverse, inv_ref.shape)
    low = (z * vec_ref[1:2] + vec_ref[2:3]).astype(BF)
    ff = hid_ref.shape[2]
    for half in range(2):
        for at in range(0, ff, 512):
            pre = mm(low, weights[half, :, width + at : width + at + 512], NN)
            gelu, slope = gelu_both(pre + bias_refs[half][:, at : at + 512])
            hid_ref[half, :, at : at + 512] = gelu.astype(BF)
            slope_ref[half, :, at : at + 512] = slope.astype(BF)


def row_tile(tile, width):
    return pl.BlockSpec((tile, width), lambda i, w: (i, 0))


def halves_tile(tile, width):
    return pl.BlockSpec((2, tile, width), lambda i, w: (0, i, 0))


ANYWHERE = pl.BlockSpec(memory_space=pl.ANY)


def first_part(where, tokens, ctx, vectors, bias, pieces, tile=256):
    d_model = tokens.shape[1]
    seq = ctx[0].shape[0]
    width, ff = ctx[0].shape[1], bias[0].shape[1]
    return pl.pallas_call(
        functools.partial(first_kernel, len(pieces)),
        out_shape=(
            jax.ShapeDtypeStruct((seq, d_model), F32),
            jax.ShapeDtypeStruct((seq, 128), F32),
            jax.ShapeDtypeStruct((2, seq, ff), BF),
            jax.ShapeDtypeStruct((2, seq, ff), BF),
        ),
        grid_spec=pltpu.PrefetchScalarGridSpec(
            num_scalar_prefetch=1,
            grid=(seq // tile,),
            in_specs=[
                own_tile(tile, d_model, seq),
                row_tile(tile, width),
                row_tile(tile, width),
                whole_spec(vectors),
                whole_spec(bias[0]),
                whole_spec(bias[1]),
            ]
            + [ANYWHERE] * len(pieces),
            out_specs=[
                row_tile(tile, d_model),
                row_tile(tile, 128),
                halves_tile(tile, ff),
                halves_tile(tile, ff),
            ],
            scratch_shapes=[
                pltpu.VMEM((2, d_model, width + ff), BF),
                pltpu.SemaphoreType.DMA((8, 4)),
            ],
        ),
        cost_estimate=cost(19.4),
        name="first_part",
    )(where, tokens, *ctx, vectors, *bias, *pieces)


def second_kernel(staged, n_down, where, hid_ref, z_ref, cot_ref, vec_ref, *refs):
    pieces = refs[:n_down]
    out_ref, own_ref, d_ref, sum_ref, keep_ref, *refs = refs[n_down:]
    weights, turned, kept, result, sem, out_sem = refs
    step = pl.program_id(0)
    tile, ff = hid_ref.shape[1:]

    @pl.when(step == 0)
    def _():
        for copy in piece_copies(where, pieces, weights, sem):
            copy.wait()
        sum_ref[...] = jnp.zeros_like(sum_ref)

    ffn = mm(hid_ref[0], weights[0], NT) + mm(hid_ref[1], weights[1], NT)
    resid = z_ref[...] * vec_ref[1:2] + vec_ref[2:3] + ffn + vec_ref[3:4]
    z, inverse = row_norm(resid)
    out = (z * vec_ref[4:5] + vec_ref[5:6]).astype(BF)
    out_ref[...] = out
    own_ref[...] = out
    cot = cot_ref[...].astype(F32)
    d_two = row_norm_back(cot, z, inverse, vec_ref[4:5])
    d_ref[...] = d_two
    sum_ref[0:1] += column_sum(cot * z)
    sum_ref[1:2] += column_sum(cot)
    sum_ref[2:3] += column_sum(d_two)
    rows = pl.ds(pl.multiple_of(step * tile, tile), tile)
    turned[:, rows] = d_two.astype(BF).T
    kept[:, rows, :] = hid_ref[...]

    @pl.when(step == pl.num_programs(0) - 1)
    def _():
        for half in range(2):
            for at in range(0, ff, 512):
                result[half, :, at : at + 512] = mm(
                    turned[...], kept[half, :, at : at + 512], NN
                ).astype(BF)
            for copy in part_copies(where, result, half, keep_ref, None, out_sem, staged):
                copy.start()
        for half in range(2):
            for copy in part_copies(where, result, half, keep_ref, None, out_sem, staged):
                copy.wait()


def second_part(where, staged, hidden, z_one, cot, vectors, pieces, tile=256):
    _, seq, ff = hidden.shape
    d_model = z_one.shape[1]
    return pl.pallas_call(
        functools.partial(second_kernel, staged, len(pieces)),
        out_shape=(
            jax.ShapeDtypeStruct((2 * seq, d_model), BF),
            jax.ShapeDtypeStruct((seq, d_model), BF),
            jax.ShapeDtypeStruct((seq, d_model), F32),
            jax.ShapeDtypeStruct((8, d_model), F32),
            (
                jax.ShapeDtypeStruct((16, 2, d_model // 16, ff), BF)
                if staged
                else jax.ShapeDtypeStruct((2, d_model, ff), BF)
            ),
        ),
        grid_spec=pltpu.PrefetchScalarGridSpec(
            num_scalar_prefetch=1,
            grid=(seq // tile,),
            in_specs=[
                halves_tile(tile, ff),
                row_tile(tile, d_model),
                own_tile(tile, d_model, seq),
                whole_spec(vectors),
            ]
            + [ANYWHERE] * len(pieces),
            out_specs=[
                own_tile(tile, d_model, seq),
                row_tile(tile, d_model),
                row_tile(tile, d_model),
                pl.BlockSpec((8, d_model), lambda i, w: (0, 0)),
                ANYWHERE,
            ],
            scratch_shapes=[
                pltpu.VMEM((2, d_model, ff), BF),
                pltpu.VMEM((d_model, seq), BF),
                pltpu.VMEM((2, seq, ff), BF),
                pltpu.VMEM((2, d_model, ff), BF),
                pltpu.SemaphoreType.DMA((8, 4)),
                pltpu.SemaphoreType.DMA((2, 16)),
            ],
        ),
        cost_estimate=cost(21.8),
        name="second_part",
    )(where, hidden, z_one, cot, vectors, *pieces)


def third_kernel(n_up, n_down, where, d_ref, slope_ref, z_ref, inv_ref, vec_ref, *refs):
    up_pieces, down_pieces, refs = refs[:n_up], refs[n_up : n_up + n_down], refs[n_up + n_down :]
    pre_ref, low_ref, one_ref, one_low_ref, ctx_ref, sum_ref, bias_ref, *refs = refs
    up, down, sem, down_sem = refs
    step = pl.program_id(0)
    ff = slope_ref.shape[2]
    width = ctx_ref.shape[2]

    @pl.when(step == 0)
    def _():
        waits = piece_copies(where, down_pieces, down, down_sem)
        waits += piece_copies(where, up_pieces, up, sem, True)
        for copy in waits:
            copy.wait()
        sum_ref[...] = jnp.zeros_like(sum_ref)
        bias_ref[...] = jnp.zeros_like(bias_ref)

    d_two = d_ref[...]
    d_two_low = d_two.astype(BF)
    d_normed = d_two
    for half in range(2):
        for at in range(0, ff, 512):
            span = slice(at, at + 512)
            d_pre = mm(d_two_low, down[half, :, span], NN) * slope_ref[half, :, span].astype(F32)
            d_pre = d_pre.astype(BF)
            pre_ref[half, :, span] = d_pre
            bias_ref[half, 0:1, span] += column_sum(d_pre.astype(F32))
            d_normed = d_normed + mm(d_pre, up[half, :, width + at : width + at + 512], NT)
    z = z_ref[...]
    low_ref[...] = (z * vec_ref[1:2] + vec_ref[2:3]).astype(BF)
    d_one = row_norm_back(d_normed, z, inv_ref[:, 0:1], vec_ref[1:2])
    one_ref[...] = d_one
    sum_ref[0:1] += column_sum(d_normed * z)
    sum_ref[1:2] += column_sum(d_normed)
    sum_ref[2:3] += column_sum(d_one)
    d_one_low = d_one.astype(BF)
    one_low_ref[...] = d_one_low
    for half in range(2):
        ctx_ref[half] = mm(d_one_low, up[half, :, :width], NN).astype(BF)


def third_part(where, d_two, slope, z_one, inv_one, vectors, up_pieces, down_pieces, width, tile=256):
    seq, d_model = d_two.shape
    ff = slope.shape[2]
    return pl.pallas_call(
        functools.partial(third_kernel, len(up_pieces), len(down_pieces)),
        out_shape=(
            jax.ShapeDtypeStruct((2, seq, ff), BF),
            jax.ShapeDtypeStruct((seq, d_model), BF),
            jax.ShapeDtypeStruct((seq, d_model), F32),
            jax.ShapeDtypeStruct((seq, d_model), BF),
            jax.ShapeDtypeStruct((2, seq, width), BF),
            jax.ShapeDtypeStruct((8, d_model), F32),
            jax.ShapeDtypeStruct((2, 8, ff), F32),
        ),
        grid_spec=pltpu.PrefetchScalarGridSpec(
            num_scalar_prefetch=1,
            grid=(seq // tile,),
            in_specs=[
                row_tile(tile, d_model),
                halves_tile(tile, ff),
                row_tile(tile, d_model),
                row_tile(tile, 128),
                whole_spec(vectors),
            ]
            + [ANYWHERE] * (len(up_pieces) + len(down_pieces)),
            out_specs=[
                halves_tile(tile, ff),
                row_tile(tile, d_model),
                row_tile(tile, d_model),
                row_tile(tile, d_model),
                halves_tile(tile, width),
                pl.BlockSpec((8, d_model), lambda i, w: (0, 0)),
                pl.BlockSpec((2, 8, ff), lambda i, w: (0, 0, 0)),
            ],
            scratch_shapes=[
                pltpu.VMEM((2, d_model, width + ff), BF),
                pltpu.VMEM((2, d_model, ff), BF),
                pltpu.SemaphoreType.DMA((8, 4)),
                pltpu.SemaphoreType.DMA((8, 4)),
            ],
        ),
        cost_estimate=cost(25.6),
        name="third_part",
    )(where, d_two, slope, z_one, inv_one, vectors, *up_pieces, *down_pieces)


def add(first, second):
    return (first.astype(F32) + second.astype(F32)).astype(BF)


def core_stage(keep, send):
    return move(send, MOVE_CORE), keep


def flip_stage(moves, got, keep):
    return move(add(keep[1], got[1]), moves), add(keep[0], got[0])


def z_stage(*terms):
    sums = [functools.reduce(jnp.add, [t[k].astype(F32) for t in terms]) for k in range(4)]
    parts = [move(part.astype(BF), moves) for part, moves in zip(sums[1:], MOVE_Z)]
    return parts, sums[0]


def z_sum(parts, keep):
    return keep + parts[0].astype(F32) + parts[1].astype(F32) + parts[2].astype(F32)


def lane_mask(head, rows):
    lanes = lax.broadcasted_iota(jnp.int32, (rows, PAIR), 1)
    return (lanes < HD) if head == 0 else (lanes >= HD)


def attn_fwd_kernel(table, qkv_ref, ctx_ref, prob_ref):
    pair = pl.program_id(0)
    q_ref, k_ref, v_ref = (qkv_ref.at[:, n * PAIR : (n + 1) * PAIR] for n in range(3))
    lanes = lax.broadcasted_iota(jnp.int32, (1, HALF), 1)
    for half in range(2):
        rows = pl.ds(half * HALF, HALF)
        query = q_ref[rows, :] * jnp.asarray(HD**-0.5, BF)
        parts = []
        for head in range(2):
            at = (pair * 2 + head) * 4
            start = (half ^ table[at]) * HALF
            flags = [table[at + 1 + n] == 1 for n in range(3)]
            key_lo = k_ref[pl.ds(pl.multiple_of(start, BLOCK), BLOCK), :]
            key_hi = k_ref[pl.ds(pl.multiple_of(start + BLOCK, BLOCK), BLOCK), :]
            masked = jnp.where(lane_mask(head, HALF), query, jnp.zeros_like(query))
            score_lo = mm(key_lo, masked, NT)
            score_hi = mm(key_hi, masked[BLOCK:], NT)
            no_lo = jnp.where(
                lanes < BLOCK,
                jnp.where(flags[0], 0.0, -1e30),
                jnp.where(flags[1], 0.0, -1e30),
            ).astype(F32)
            no_hi = jnp.where(flags[2], 0.0, -1e30).astype(F32)
            top_lo = jnp.max(score_lo, axis=0, keepdims=True) + no_lo
            top_hi = jnp.max(score_hi, axis=0, keepdims=True) + no_hi
            top = jnp.concatenate(
                [top_lo[:, :BLOCK], jnp.maximum(top_lo[:, BLOCK:], top_hi)], axis=1
            )
            ref_lo = jnp.where(no_lo < 0.0, 1e30, top)
            ref_hi = jnp.where(no_hi < 0.0, 1e30, top[:, BLOCK:])
            exp_lo = jnp.exp(score_lo - ref_lo)
            exp_hi = jnp.exp(score_hi - ref_hi)
            sum_lo = jnp.sum(exp_lo, axis=0, keepdims=True)
            sum_hi = jnp.sum(exp_hi, axis=0, keepdims=True)
            total = jnp.concatenate([sum_lo[:, :BLOCK], sum_lo[:, BLOCK:] + sum_hi], axis=1)
            scale = jnp.where(total > 0.0, 1.0 / jnp.where(total > 0.0, total, 1.0), 0.0)
            prob_lo = (exp_lo * scale).astype(BF)
            prob_hi = (exp_hi * scale[:, BLOCK:]).astype(BF)
            prob_ref[0, head, half, :, :HALF] = prob_lo
            prob_ref[0, head, half, :, HALF:] = prob_hi
            val_lo = v_ref[pl.ds(pl.multiple_of(start, BLOCK), BLOCK), :].T
            val_hi = v_ref[pl.ds(pl.multiple_of(start + BLOCK, BLOCK), BLOCK), :].T
            side = slice(head * HD, (head + 1) * HD)
            out_lo = mm(val_lo[side], prob_lo, NN)
            out_hi = mm(val_hi[side], prob_hi, NN)
            parts.append(
                jnp.concatenate([out_lo[:, :BLOCK], out_lo[:, BLOCK:] + out_hi], axis=1)
            )
        ctx_ref[rows, :] = jnp.concatenate(parts, axis=0).T.astype(BF)


def attn_fwd(table, proj):
    seq, width = proj.shape
    pairs = width // 3 // PAIR
    return pl.pallas_call(
        attn_fwd_kernel,
        out_shape=(
            jax.ShapeDtypeStruct((seq, width // 3), BF),
            jax.ShapeDtypeStruct((pairs, 2, 2, BLOCK, HALF + BLOCK), BF),
        ),
        grid_spec=pltpu.PrefetchScalarGridSpec(
            num_scalar_prefetch=1,
            grid=(pairs,),
            in_specs=[pl.BlockSpec((seq, 3 * PAIR), lambda p, t: (0, p))],
            out_specs=[
                pl.BlockSpec((seq, PAIR), lambda p, t: (0, p)),
                pl.BlockSpec((1, 2, 2, BLOCK, HALF + BLOCK), lambda p, t: (p, 0, 0, 0, 0)),
            ],
        ),
        cost_estimate=cost(0.5),
        name="attn_fwd",
    )(table, proj)


def attn_bwd_kernel(table, qkv_ref, d_ref, prob_ref, out_ref, sum_ref, k_acc, v_acc):
    pair = pl.program_id(0)
    q_ref, k_ref, v_ref = (qkv_ref.at[:, n * PAIR : (n + 1) * PAIR] for n in range(3))
    for half in range(2):
        rows = pl.ds(half * HALF, HALF)
        query = q_ref[rows, :] * jnp.asarray(HD**-0.5, BF)
        d_ctx = d_ref[rows, :]
        parts = []
        for head in range(2):
            at = (pair * 2 + head) * 4
            start = (half ^ table[at]) * HALF
            at_lo = pl.ds(pl.multiple_of(start, BLOCK), BLOCK)
            at_hi = pl.ds(pl.multiple_of(start + BLOCK, BLOCK), BLOCK)
            keep = lane_mask(head, HALF)
            query_h = jnp.where(keep, query, jnp.zeros_like(query))
            d_ctx_h = jnp.where(keep, d_ctx, jnp.zeros_like(d_ctx))
            prob_lo = prob_ref[0, head, half, :, :HALF]
            prob_hi = prob_ref[0, head, half, :, HALF:]
            d_w_lo = mm(v_ref[at_lo, :], d_ctx_h, NT)
            d_w_hi = mm(v_ref[at_hi, :], d_ctx_h[BLOCK:], NT)
            wide_lo = prob_lo.astype(F32)
            wide_hi = prob_hi.astype(F32)
            dot_lo = jnp.sum(wide_lo * d_w_lo, axis=0, keepdims=True)
            dot_hi = jnp.sum(wide_hi * d_w_hi, axis=0, keepdims=True)
            dot = jnp.concatenate([dot_lo[:, :BLOCK], dot_lo[:, BLOCK:] + dot_hi], axis=1)
            d_s_lo = (wide_lo * (d_w_lo - dot)).astype(BF)
            d_s_hi = (wide_hi * (d_w_hi - dot[:, BLOCK:])).astype(BF)
            dk_lo = mm(d_s_lo, query_h, NN)
            dk_hi = mm(d_s_hi, query_h[BLOCK:], NN)
            dv_lo = mm(prob_lo, d_ctx_h, NN)
            dv_hi = mm(prob_hi, d_ctx_h[BLOCK:], NN)
            k_acc[head, at_lo, :] = dk_lo
            k_acc[head, at_hi, :] = dk_hi
            v_acc[head, at_lo, :] = dv_lo
            v_acc[head, at_hi, :] = dv_hi
            key_lo = k_ref[at_lo, :].T
            key_hi = k_ref[at_hi, :].T
            side = slice(head * HD, (head + 1) * HD)
            dq_lo = mm(key_lo[side], d_s_lo, NN)
            dq_hi = mm(key_hi[side], d_s_hi, NN)
            parts.append(jnp.concatenate([dq_lo[:, :BLOCK], dq_lo[:, BLOCK:] + dq_hi], axis=1))
        out_ref[rows, :PAIR] = (jnp.concatenate(parts, axis=0).T * HD**-0.5).astype(BF)
    out_ref[:, PAIR : 2 * PAIR] = (k_acc[0] + k_acc[1]).astype(BF)
    out_ref[:, 2 * PAIR :] = (v_acc[0] + v_acc[1]).astype(BF)
    sums = jnp.sum(out_ref[...].astype(F32), axis=0, keepdims=True)
    sum_ref[0] = jnp.broadcast_to(sums, sum_ref.shape[1:])


def attn_bwd(table, proj, d_context, half, probs):
    seq, width = proj.shape
    pairs = width // 3 // PAIR
    return pl.pallas_call(
        attn_bwd_kernel,
        out_shape=(
            jax.ShapeDtypeStruct((seq, width), BF),
            jax.ShapeDtypeStruct((pairs, 8, 3 * PAIR), F32),
        ),
        grid_spec=pltpu.PrefetchScalarGridSpec(
            num_scalar_prefetch=1,
            grid=(pairs,),
            in_specs=[
                pl.BlockSpec((seq, 3 * PAIR), lambda p, t: (0, p)),
                pl.BlockSpec((None, seq, PAIR), lambda p, t: (half, 0, p)),
                pl.BlockSpec((1, 2, 2, BLOCK, HALF + BLOCK), lambda p, t: (p, 0, 0, 0, 0)),
            ],
            out_specs=[
                pl.BlockSpec((seq, 3 * PAIR), lambda p, t: (0, p)),
                pl.BlockSpec((1, 8, 3 * PAIR), lambda p, t: (p, 0, 0)),
            ],
            scratch_shapes=[pltpu.VMEM((2, seq, PAIR), F32)] * 2,
        ),
        cost_estimate=cost(11.3),
        name="attn_bwd",
    )(table, proj, d_context, probs)


def gelu_both(values):
    half = 0.5 * (1.0 + lax.erf(values * (0.5**0.5)))
    slope = half + values * jnp.exp(-0.5 * values * values) * 0.3989422804014327
    return values * half, slope


def body(
    dp_size,
    tokens,
    grad_out,
    head_perm,
    block_mask,
    w_qkv,
    b_qv,
    w_out,
    b_out,
    gain_one,
    shift_one,
    w_up,
    b_up,
    w_down,
    b_down,
    gain_two,
    shift_two,
):
    seq = tokens.shape[0] // head_perm.shape[0]
    rows = w_qkv.shape[0]
    width = w_qkv.shape[2]
    d_model = tokens.shape[1]
    dp_at = lax.axis_index("dp")
    mp_at = lax.axis_index("mp")
    where = jnp.stack([dp_at // 4, (dp_at // 2) % 2, dp_at % 2, mp_at]).astype(jnp.int32)

    table = jnp.concatenate([head_perm[:, :, None], block_mask], axis=2).astype(jnp.int32)
    table = table.reshape(2, -1)
    table_own = lax.dynamic_index_in_dim(table, mp_at, 0, keepdims=False)
    table_other = swap_mp(lax.dynamic_index_in_dim(table, 1 - mp_at, 0, keepdims=False))

    small = jnp.stack(
        [
            b_out,
            gain_one,
            shift_one,
            b_down,
            gain_two,
            shift_two,
            b_up[:rows],
            b_up[rows:],
            b_qv.reshape(-1),
        ],
        axis=1,
    )
    small = jnp.pad(small, ((0, 0), (0, SMALL - small.shape[1])))
    pairs = width // PAIR
    by_pair = w_qkv.reshape(rows, 3, pairs, PAIR).transpose(0, 2, 1, 3).reshape(rows, 3 * width)
    shard_qkv = jnp.concatenate([by_pair, small], axis=1)
    shard_up = jnp.concatenate([w_out.T, w_up], axis=1)
    shard_down = w_down.T
    staged = dp_size == 16

    def plain_gather(shard):
        full = lax.all_gather(shard, "dp", axis=0, tiled=True)
        return full, swap_mp(full)

    def gather_z(shard):
        return jnp.stack([shard] + [move(shard, moves) for moves in MOVE_Z])

    def gather_core(*pieces):
        return (*pieces, *(move(piece, MOVE_CORE) for piece in pieces))

    if staged:
        qkv_z = gather_z(shard_qkv)
        qkv_y = move(qkv_z, MOVE_Y)
        qkv_x = move(qkv_z, MOVE_X)
        up_parts = [move(after(shard_up, qkv_z), moves) for moves in MOVE_Z]
        down_whole = lax.all_gather(after(shard_down, qkv_z), AXES)
        down_pieces = (down_whole.reshape(dp_size, 2, *shard_down.shape),)
        qkv_y, *up_parts = lax.optimization_barrier((qkv_y, *up_parts))
        qkv_own = gather_core(qkv_z, qkv_y)
        qkv_xy = move(qkv_y, MOVE_X)
        up_z = jnp.stack([shard_up, *up_parts])
        tokens_in, table_other, qkv_x, up_z = lax.optimization_barrier(
            (tokens, table_other, qkv_x, up_z)
        )
        up_a, up_b = move(up_z, MOVE_FIRST), move(up_z, MOVE_SECOND)
    else:
        qkv_own, qkv_other = ((piece,) for piece in plain_gather(shard_qkv))
        up_pieces = plain_gather(shard_up)
        down_pieces = plain_gather(shard_down)
        tokens_in = tokens

    ff = w_up.shape[1]

    def project_half(values, pieces):
        return project(where, values, pieces, rows, seq, 3 * width, ff)

    proj_own, vectors, bias_own = project_half(tokens_in, qkv_own)
    if staged:
        proj_own, qkv_xy = lax.optimization_barrier((proj_own, qkv_xy))
        qkv_other = gather_core(qkv_x, qkv_xy)
    ctx_own, probs_own = attn_fwd(table_own, proj_own)
    if staged:
        ctx_own, up_a = lax.optimization_barrier((ctx_own, up_a))
    proj_other, _, bias_other = project_half(after(tokens, ctx_own), qkv_other)
    if staged:
        proj_other, up_a = lax.optimization_barrier((proj_other, up_a))
        up_c = move(up_a, MOVE_SECOND)
        up_pieces = gather_core(up_z, up_a, up_b)
    ctx_other, probs_other = attn_fwd(table_other, proj_other)
    if staged:
        ctx_other, up_c = lax.optimization_barrier((ctx_other, up_c))
        up_pieces = (*up_pieces[:3], up_c, *up_pieces[3:], move(up_c, MOVE_CORE))
    tables, proj = (table_own, table_other), (proj_own, proj_other)
    probs = (probs_own, probs_other)
    ctx = (ctx_own, ctx_other)
    qkv_pieces = (*qkv_own, *qkv_other)
    z_one, inv_one, hidden, slope = first_part(
        where, tokens, ctx, vectors, (bias_own, bias_other), up_pieces
    )

    def place(whole, other):
        return lax.dynamic_update_slice_in_dim(
            whole, other.astype(whole.dtype), (1 - mp_at) * seq, 0
        )

    out_whole, out_own, d_two, sums_two, down_grad = second_part(
        where, staged, hidden, z_one, grad_out, vectors, down_pieces
    )
    out_other = swap_mp(out_own)

    def plain_scatter(own, other):
        summed = own.astype(F32) + swap_mp(other).astype(F32)
        return lax.psum_scatter(summed, "dp", scatter_dimension=0, tiled=True)

    if staged:
        down_grad = down_grad.reshape(2 * dp_size, *shard_down.shape)
        s_down = lax.psum_scatter(down_grad, AXES, scatter_dimension=0).astype(F32)
    else:
        s_down = plain_scatter(*down_grad)
    d_pre, normed_low, d_one, d_one_low, d_ctx, sums_one, sums_up = third_part(
        where, d_two, slope, z_one, inv_one, vectors, up_pieces, down_pieces, width
    )
    up_parts = grads(
        where,
        staged,
        rows,
        [normed_low, d_one_low],
        [(d_pre, d_pre), ctx],
        (sums_two, sums_one, sums_up),
    )
    d_ctx_other = d_ctx
    if staged:
        up_got, up_keep = core_stage(*up_parts)
        d_ctx_other, out_other, up_keep = lax.optimization_barrier((d_ctx, out_other, up_keep))
    else:
        s_up = plain_scatter(*up_parts[0])
    d_proj_other, sums_other = attn_bwd(tables[1], proj[1], d_ctx_other, 1, probs[1])
    if staged:
        d_proj_other, up_got = lax.optimization_barrier((d_proj_other, up_got))
        up_got, up_keep = flip_stage(MOVE_REDUCE[0], up_got, up_keep)
        d_proj_other, up_keep = lax.optimization_barrier((d_proj_other, up_keep))
    other_parts = grads(where, staged, rows, [tokens], [(d_proj_other,)], (sums_other,))
    d_ctx_own = d_ctx
    if staged:
        qo_got, qo_keep = core_stage(*other_parts)
        d_ctx_own, qo_keep = lax.optimization_barrier((d_ctx, qo_keep))
    d_proj_own, sums_own = attn_bwd(tables[0], proj[0], d_ctx_own, 0, probs[0])
    d_proj_last = d_proj_own
    if staged:
        d_proj_own, up_got, qo_got = lax.optimization_barrier((d_proj_own, up_got, qo_got))
        up_got, up_keep = flip_stage(MOVE_REDUCE[1], up_got, up_keep)
        qo_got, qo_keep = flip_stage(MOVE_Y, qo_got, qo_keep)
        d_proj_last, up_keep, qo_keep = lax.optimization_barrier((d_proj_own, up_keep, qo_keep))
    d_input, in_low = last_part(where, (d_proj_last, d_proj_other), d_one, qkv_pieces)
    tokens_in = tokens
    if staged:
        in_both = lax.all_gather(in_low, "mp")
        tokens_in, in_low, up_got, qo_got = lax.optimization_barrier(
            (tokens, in_low, up_got, qo_got)
        )
        qo_in = move(add(qo_keep, qo_got), MOVE_X)
        up_parts, up_keep = z_stage(up_got, up_keep)
        tokens_in, up_keep = lax.optimization_barrier((tokens_in, up_keep))
    else:
        in_other = swap_mp(in_low)
    own_parts = grads(where, staged, rows, [tokens_in], [(d_proj_own,)], (sums_own,))
    if staged:
        qs_got, qs_keep = core_stage(*own_parts)
        qs_keep, *up_parts = lax.optimization_barrier((qs_keep, *up_parts))
        qs_got, qs_keep = flip_stage(MOVE_Y, qs_got, qs_keep)
        s_up = z_sum(up_parts, up_keep)
        qs_parts, qs_keep = z_stage(qs_got, qs_keep, qo_in)
        s_qkv = z_sum(qs_parts, qs_keep)[0]
        in_both, s_qkv = lax.optimization_barrier((in_both, s_qkv))
        in_other = lax.dynamic_index_in_dim(in_both, 1 - mp_at, 0, keepdims=False)
        d_input = place(d_input, in_other)
    else:
        d_input = place(d_input, in_other)
        s_qkv = plain_scatter(own_parts[0][0], other_parts[0][0])

    cols = s_up[:, ff + width :].T
    g_w_qkv = s_qkv[:, : 3 * width].reshape(rows, pairs, 3, PAIR).transpose(0, 2, 1, 3)
    return (
        place(out_whole, out_other),
        d_input,
        g_w_qkv.reshape(rows, 3, width),
        s_qkv[:, 3 * width].reshape(2, rows // 2),
        s_up[:, ff : ff + width].T,
        cols[0],
        cols[1],
        cols[2],
        s_up[:, :ff],
        cols[6:8].reshape(-1),
        s_down.T,
        cols[3],
        cols[4],
        cols[5],
    )


def solution(mesh):
    placed = (
        P("dp", None),
        P("dp", None),
        P("dp", "mp"),
        P("dp", "mp", None),
        P("dp", None, "mp"),
        P(None, ("mp", "dp")),
        P("mp", "dp"),
        P("dp"),
        P("dp"),
        P("dp"),
        P("dp", "mp"),
        P(("mp", "dp")),
        P("mp", "dp"),
        P("dp"),
        P("dp"),
        P("dp"),
    )
    return jax.shard_map(
        functools.partial(body, mesh.shape["dp"]),
        mesh=mesh,
        in_specs=placed,
        out_specs=(
            P("dp", None),
            P("dp", None),
            P("dp", None, "mp"),
            P(None, ("mp", "dp")),
            P("mp", "dp"),
            P("dp"),
            P("dp"),
            P("dp"),
            P("dp", "mp"),
            P(("mp", "dp")),
            P("mp", "dp"),
            P("dp"),
            P("dp"),
            P("dp"),
        ),
        check_vma=False,
    )
```

profile of v0, /device:TPU:0, one launch (start us, length us, event | category | flops | bytes accessed | tf_op | source)
XLA Modules:
  0.0 329.1 jit_solution(4043733908206338339)
XLA Ops:
  10.8 4.1 %collective-permute-start.2 = (bf16[48,1280]{1,0:T(8,128)(2,1)S(1)}, bf16[48,1280]{1,0:T(8,128)(2,1)S(1)}, u32[]{:S(2)}, u32[]{:S(2)}) collective-permute-start(bf16[48,1280]{1,0:T(8,128)(2,1)S(1)} %get-tuple-element.200), channel_id=1, source_target_pairs={{0,16},{1,17},{2,18},{3,19},{4,20},{5,21},{6,22},{7,23},{8,24},{9,... | collective-permute-start | bytes 368648 | tf_op jit(solution)/shard_map/ppermute | solution.py:57
  18.8 5.7 %collective-permute-done.2 = bf16[48,1280]{1,0:T(8,128)(2,1)S(1)} collective-permute-done((bf16[48,1280]{1,0:T(8,128)(2,1)S(1)}, bf16[48,1280]{1,0:T(8,128)(2,1)S(1)}, u32[]{:S(2)}, u32[]{:S(2)}) %collective-permute-start.2) | collective-permute-done | bytes 122912 | tf_op jit(solution)/shard_map/ppermute | solution.py:57
  35.9 11.9 %collective-permute-done.7 = bf16[48,1920]{1,0:T(8,128)(2,1)S(1)} collective-permute-done((bf16[48,1920]{1,0:T(8,128)(2,1)S(1)}, bf16[48,1920]{1,0:T(8,128)(2,1)S(1)}, u32[]{:S(2)}, u32[]{:S(2)}) %collective-permute-start.7) | collective-permute-done | bytes 184352 | tf_op jit(solution)/shard_map/ppermute | solution.py:57
  55.4 8.7 %project.2 = (bf16[1024,1152]{1,0:T(8,128)(2,1)}, f32[8,768]{1,0:T(8,128)}, f32[1,1536]{1,0:T(1,128)}) custom-call(s32[4]{0:T(128)} %pad_add_fusion.1.where, bf16[2048,768]{1,0:T(8,128)(2,1)} %refs_0_.2, bf16[4,48,1280]{2,1,0:T(8,128)(2,1)} %copy-done.4, bf16[4,48,1280]{2,1,0:T(8,128)(2,1)} %copy-done.11, bf16[4,48,1280]{2,1,0:T(8,128)(2,1)} %copy-done.12, ...), custom_call_target="tpu_custom_call" | custom-call | flops 34800001024 | bytes 104400000 | tf_op jit(solution)/shard_map/project/pallas_call | solution.py:187
  65.8 8.9 %attn_fwd.2 = (bf16[1024,384]{1,0:T(8,128)(2,1)}, bf16[3,2,2,256,768]{4,3,2,1,0:T(8,128)(2,1)}) custom-call(s32[24]{0:T(128)} %get-tuple-element.202.table, bf16[1024,1152]{1,0:T(8,128)(2,1)} %get-tuple-element.103.qkv_ref), custom_call_target="tpu_custom_call" | custom-call | flops 2000000000 | bytes 6000000 | tf_op jit(solution)/shard_map/attn_fwd/pallas_call | solution.py:753
  74.7 3.4 %collective-permute-done.12.refs_1_ = bf16[4,48,1920]{2,1,0:T(8,128)(2,1)S(1)} collective-permute-done((bf16[4,48,1920]{2,1,0:T(8,128)(2,1)S(1)}, bf16[4,48,1920]{2,1,0:T(8,128)(2,1)S(1)}, u32[]{:S(2)}, u32[]{:S(2)}) %collective-permute-start.12) | collective-permute-done | bytes 737312 | tf_op jit(solution)/shard_map/ppermute | solution.py:57
  79.0 8.6 %project.3 = (bf16[1024,1152]{1,0:T(8,128)(2,1)}, f32[8,768]{1,0:T(8,128)}, f32[1,1536]{1,0:T(1,128)}) custom-call(s32[4]{0:T(128)} %pad_add_fusion.1.where, bf16[2048,768]{1,0:T(8,128)(2,1)} %refs_0_.2, bf16[4,48,1280]{2,1,0:T(8,128)(2,1)} %collective-permute-done.4.refs_0_.refs_4_, bf16[4,48,1280]{2,1,0:T(8,128)(2,1)} %collective-permute-done.11.refs_1_.refs_5_, ...), custom_call_target="tpu_custom_call" | custom-call | flops 34800001024 | bytes 104400000 | tf_op jit(solution)/shard_map/project/pallas_call | solution.py:187
  88.8 8.9 %attn_fwd.3 = (bf16[1024,384]{1,0:T(8,128)(2,1)}, bf16[3,2,2,256,768]{4,3,2,1,0:T(8,128)(2,1)}) custom-call(s32[24]{0:T(128)} %copy-done.14, bf16[1024,1152]{1,0:T(8,128)(2,1)} %get-tuple-element.113.qkv_ref), custom_call_target="tpu_custom_call" | custom-call | flops 2000000000 | bytes 6000000 | tf_op jit(solution)/shard_map/attn_fwd/pallas_call | solution.py:753
  102.0 20.1 %first_part.1 = (f32[1024,768]{1,0:T(8,128)}, f32[1024,128]{1,0:T(8,128)}, bf16[2,1024,1536]{2,1,0:T(8,128)(2,1)}, bf16[2,1024,1536]{2,1,0:T(8,128)(2,1)}) custom-call(s32[4]{0:T(128)} %pad_add_fusion.1.where, bf16[2048,768]{1,0:T(8,128)(2,1)} %refs_0_.2, bf16[1024,384]{1,0:T(8,128)(2,1)} %get-tuple-element.106.ctx0_ref.refs_4_, ...), custom_call_target="tpu_custom_call" | custom-call | flops 77599997952 | bytes 232800000 | tf_op jit(solution)/shard_map/first_part/pallas_call | solution.py:459
  122.1 3.4 %all-gather.5.cloned.1.call-done = bf16[1536,1536]{1,0:T(8,128)(2,1)} async-done(((bf16[48,1536]{1,0:T(8,128)(2,1)}), bf16[1536,1536]{1,0:T(8,128)(2,1)}) %all-gather.5.cloned.1.call-update) | async-done | bytes 4718608 | tf_op jit(solution)/shard_map/all_gather | solution.py:924
  125.5 21.9 %second_part.1 = (bf16[2048,768]{1,0:T(8,128)(2,1)}, bf16[1024,768]{1,0:T(8,128)(2,1)}, f32[1024,768]{1,0:T(8,128)}, f32[8,768]{1,0:T(8,128)}, bf16[16,2,48,1536]{3,2,1,0:T(8,128)(2,1)}) custom-call(s32[4]{0:T(128)} %pad_add_fusion.1.where, bf16[2,1024,1536]{2,1,0:T(8,128)(2,1)} %get-tuple-element.121.hid_ref, f32[1024,768]{1,0:T(8,128)} %get-tuple-element.122.z_ref, ...), custom_call_target="tpu_custom_call" | custom-call | flops 87199997952 | bytes 261600000 | tf_op jit(solution)/shard_map/second_part/pallas_call | solution.py:541
  149.0 26.3 %third_part.1 = (bf16[2,1024,1536]{2,1,0:T(8,128)(2,1)}, bf16[1024,768]{1,0:T(8,128)(2,1)}, f32[1024,768]{1,0:T(8,128)}, bf16[1024,768]{1,0:T(8,128)(2,1)}, bf16...) custom-call(s32[4]{0:T(128)} %pad_add_fusion.1.where, f32[1024,768]{1,0:T(8,128)} %get-tuple-element.125.d_ref, ...), custom_call_target="tpu_custom_call" | custom-call | flops 102400000000 | bytes 307200000 | tf_op jit(solution)/shard_map/third_part/pallas_call | solution.py:629
  175.3 20.4 %grads.3 = (bf16[2,2,4,48,2048]{4,3,2,1,0:T(8,128)(2,1)}, bf16[2,2,4,48,2048]{4,3,2,1,0:T(8,128)(2,1)}) custom-call(s32[4]{0:T(128)} %pad_add_fusion.1.where, bf16[1024,768]{1,0:T(8,128)(2,1)} %get-tuple-element.130.refs_0_, bf16[1024,768]{1,0:T(8,128)(2,1)} %get-tuple-element.131.refs_1_, bf16[2,1024,1536]{2,1,0:T(8,128)(2,1)} %get-tuple-element.132.refs_2_.refs_3_, ...), custom_call_target="tpu_custom_call" | custom-call | flops 80000000000 | bytes 240000000 | tf_op jit(solution)/shard_map/grads/pallas_call | solution.py:375
  198.5 11.3 %attn_bwd.2 = (bf16[1024,1152]{1,0:T(8,128)(2,1)}, f32[3,8,384]{2,1,0:T(8,128)}) custom-call(s32[24]{0:T(128)} %copy-done.14, bf16[1024,1152]{1,0:T(8,128)(2,1)} %get-tuple-element.113.qkv_ref, bf16[2,1024,384]{2,1,0:T(8,128)(2,1)} %get-tuple-element.148.d_ref, bf16[3,2,2,256,768]{4,3,2,1,0:T(8,128)(2,1)} %get-tuple-element.139.prob_ref), custom_call_target="tpu_custom_call" | custom-call | flops 45199998976 | bytes 135600000 | tf_op jit(solution)/shard_map/attn_bwd/pallas_call | solution.py:824
  211.5 5.6 %fusion.1 = (bf16[2,4,48,2048]{3,2,1,0:T(8,128)(2,1)}, bf16[2,4,48,2048]{3,2,1,0:T(8,128)(2,1)S(1)}) fusion(bf16[2,2,4,48,2048]{4,3,2,1,0:T(8,128)(2,1)} %copy-done, bf16[2,2,4,48,2048]{4,3,2,1,0:T(8,128)(2,1)} %get-tuple-element.143), kind=kLoop, calls=%fused_computation.4 | loop fusion | flops 6291456 | bytes 9437184 | tf_op jit(solution)/shard_map/convert_element_type | solution.py:673
  217.8 7.4 %grads.4 = (bf16[2,4,1,48,1280]{4,3,2,1,0:T(8,128)(2,1)}, bf16[2,4,1,48,1280]{4,3,2,1,0:T(8,128)(2,1)}) custom-call(s32[4]{0:T(128)} %pad_add_fusion.1.where, bf16[2048,768]{1,0:T(8,128)(2,1)} %refs_0_.2, bf16[1024,1152]{1,0:T(8,128)(2,1)} %get-tuple-element.145.refs_1_.other_ref, f32[3,8,384]{2,1,0:T(8,128)} %get-tuple-element.146.refs_2_), custom_call_target="tpu_custom_call" | custom-call | flops 28800000000 | bytes 86400000 | tf_op jit(solution)/shard_map/grads/pallas_call | solution.py:375
  225.3 11.1 %attn_bwd.3 = (bf16[1024,1152]{1,0:T(8,128)(2,1)}, f32[3,8,384]{2,1,0:T(8,128)}) custom-call(s32[24]{0:T(128)} %get-tuple-element.202.table, bf16[1024,1152]{1,0:T(8,128)(2,1)} %get-tuple-element.103.qkv_ref, bf16[2,1024,384]{2,1,0:T(8,128)(2,1)} %get-tuple-element.148.d_ref, bf16[3,2,2,256,768]{4,3,2,1,0:T(8,128)(2,1)} %get-tuple-element.149.prob_ref), custom_call_target="tpu_custom_call" | custom-call | flops 45199998976 | bytes 135600000 | tf_op jit(solution)/shard_map/attn_bwd/pallas_call | solution.py:824
  236.4 5.5 %collective-permute-done.23 = bf16[2,4,48,2048]{3,2,1,0:T(8,128)(2,1)} collective-permute-done((bf16[2,4,48,2048]{3,2,1,0:T(8,128)(2,1)}, bf16[2,4,48,2048]{3,2,1,0:T(8,128)(2,1)}, u32[]{:S(2)}, u32[]{:S(2)}) %collective-permute-start.23) | collective-permute-done | bytes 1572896 | tf_op jit(solution)/shard_map/ppermute | solution.py:57
  248.2 11.5 %last_part.1 = (f32[2048,768]{1,0:T(8,128)}, bf16[1024,768]{1,0:T(8,128)(2,1)}) custom-call(s32[4]{0:T(128)} %pad_add_fusion.1.where, bf16[1024,1152]{1,0:T(8,128)(2,1)} %get-tuple-element.157.own_ref.refs_1_, bf16[1024,1152]{1,0:T(8,128)(2,1)} %get-tuple-element.145.refs_1_.other_ref, f32[1024,768]{1,0:T(8,128)} %get-tuple-element.158.one_ref, ...), custom_call_target="tpu_custom_call" | custom-call | flops 48000000000 | bytes 144000000 | tf_op jit(solution)/shard_map/last_part/pallas_call | solution.py:236
  266.6 7.6 %grads.5 = (bf16[2,4,1,48,1280]{4,3,2,1,0:T(8,128)(2,1)}, bf16[2,4,1,48,1280]{4,3,2,1,0:T(8,128)(2,1)}) custom-call(s32[4]{0:T(128)} %pad_add_fusion.1.where, bf16[2048,768]{1,0:T(8,128)(2,1)} %refs_0_.2, bf16[1024,1152]{1,0:T(8,128)(2,1)} %get-tuple-element.157.own_ref.refs_1_, f32[3,8,384]{2,1,0:T(8,128)} %get-tuple-element.165.refs_2_), custom_call_target="tpu_custom_call" | custom-call | flops 28800000000 | bytes 86400000 | tf_op jit(solution)/shard_map/grads/pallas_call | solution.py:375
  274.1 4.3 %collective-permute-start.30 = (bf16[2,4,1,48,1280]{4,3,2,1,0:T(8,128)(2,1)}, bf16[2,4,1,48,1280]{4,3,2,1,0:T(8,128)(2,1)}, u32[]{:S(2)}, u32[]{:S(2)}) collective-permute-start(bf16[2,4,1,48,1280]{4,3,2,1,0:T(8,128)(2,1)} %get-tuple-element.168), channel_id=1, source_target_pairs={{0,2},{1,3},{2,0},{3,1},{4,6},{5,7},{6,4},{7,5},{8,10},{9,11},{10,... | collective-permute-start | bytes 2949128 | tf_op jit(solution)/shard_map/ppermute | solution.py:57
  289.9 9.5 %collective-permute-done.31 = bf16[4,1,48,1280]{3,2,1,0:T(8,128)(2,1)S(1)} collective-permute-done((bf16[4,1,48,1280]{3,2,1,0:T(8,128)(2,1)S(1)}, bf16[4,1,48,1280]{3,2,1,0:T(8,128)(2,1)S(1)}, u32[]{:S(2)}, u32[]{:S(2)}) %collective-permute-start.31) | collective-permute-done | bytes 491552 | tf_op jit(solution)/shard_map/ppermute | solution.py:57
  310.6 5.7 %collective-permute-done.34 = bf16[1,48,1280]{2,1,0:T(8,128)(2,1)S(1)} collective-permute-done((bf16[1,48,1280]{2,1,0:T(8,128)(2,1)S(1)}, bf16[1,48,1280]{2,1,0:T(8,128)(2,1)S(1)}, u32[]{:S(2)}, u32[]{:S(2)}) %collective-permute-start.34) | collective-permute-done | bytes 122912 | tf_op jit(solution)/shard_map/ppermute | solution.py:57
  319.0 3.3 %convert_dynamic-update-slice_fusion = f32[2048,768]{1,0:T(8,128)} fusion(f32[2048,768]{1,0:T(8,128)} %get-tuple-element.159, s32[]{:T(128)S(6)} %select_n.37, bf16[2,1024,768]{2,1,0:T(8,128)(2,1)} %bitcast.123, s32[]{:T(128)S(6)} %select_n.36), kind=kLoop, calls=%fused_computation | loop fusion | flops 786432 | bytes 4718600 | tf_op jit(solution)/shard_map/dynamic_update_slice | solution.py:970
  (142 shorter events, 79.6 us)
Async XLA Ops:
  7.2 118.3 %all-gather.5.cloned.1.call-start = ((), (), s32[]{:S(2)}) async-start(), calls=%async_computation.2 | async-start | bytes 4866048 | tf_op jit(solution)/shard_map/all_gather | solution.py:924
  10.8 13.6 %collective-permute-start.2 = (bf16[48,1280]{1,0:T(8,128)(2,1)S(1)}, bf16[48,1280]{1,0:T(8,128)(2,1)S(1)}, u32[]{:S(2)}, u32[]{:S(2)}) collective-permute-start(bf16[48,1280]{1,0:T(8,128)(2,1)S(1)} %get-tuple-element.200), channel_id=1, source_target_pairs={{0,16},{1,17},{2,18},{3,19},{4,20},{5,21},{6,22},{7,23},{8,24},{9,... | collective-permute-start | bytes 368648 | tf_op jit(solution)/shard_map/ppermute | solution.py:57
  25.2 22.7 %collective-permute-start.5 = (bf16[4,48,1280]{2,1,0:T(8,128)(2,1)S(1)}, bf16[4,48,1280]{2,1,0:T(8,128)(2,1)S(1)}, u32[]{:S(2)}, u32[]{:S(2)}) collective-permute-start(bf16[4,48,1280]{2,1,0:T(8,128)(2,1)S(1)} %pad_maximum_fusion.1.refs_0_), channel_id=1, source_target_pairs={{0,4},{1,5},{2,6},{3,7},{4,0},{5,1},{6,2},{7,3},{8,12},{9,13},{10,... | collective-permute-start | bytes 1474568 | tf_op jit(solution)/shard_map/ppermute | solution.py:57
  29.9 18.0 %collective-permute-start.7 = (bf16[48,1920]{1,0:T(8,128)(2,1)S(1)}, bf16[48,1920]{1,0:T(8,128)(2,1)S(1)}, u32[]{:S(2)}, u32[]{:S(2)}) collective-permute-start(bf16[48,1920]{1,0:T(8,128)(2,1)S(1)} %get-tuple-element.96), channel_id=1, source_target_pairs={{0,16},{1,17},{2,18},{3,19},{4,20},{5,21},{6,22},{7,23},{8,24},{9,... | collective-permute-start | bytes 552968 | tf_op jit(solution)/shard_map/ppermute | solution.py:57
  31.6 16.3 %collective-permute-start.6 = (bf16[48,1920]{1,0:T(8,128)(2,1)S(1)}, bf16[48,1920]{1,0:T(8,128)(2,1)S(1)}, u32[]{:S(2)}, u32[]{:S(2)}) collective-permute-start(bf16[48,1920]{1,0:T(8,128)(2,1)S(1)} %get-tuple-element.96), channel_id=1, source_target_pairs={{0,8},{1,9},{2,10},{3,11},{4,12},{5,13},{6,14},{7,15},{8,16},{9,17... | collective-permute-start | bytes 552968 | tf_op jit(solution)/shard_map/ppermute | solution.py:57
  33.5 21.1 %collective-permute-start.9 = (bf16[4,48,1280]{2,1,0:T(8,128)(2,1)S(1)}, bf16[4,48,1280]{2,1,0:T(8,128)(2,1)S(1)}, u32[]{:S(2)}, u32[]{:S(2)}) collective-permute-start(bf16[4,48,1280]{2,1,0:T(8,128)(2,1)S(1)} %pad_maximum_fusion.1.refs_0_), channel_id=1, source_target_pairs={{0,2},{1,3},{2,0},{3,1},{4,6},{5,7},{6,4},{7,5},{8,10},{9,11},{10,... | collective-permute-start | bytes 1474568 | tf_op jit(solution)/shard_map/ppermute | solution.py:57
  34.5 18.6 %collective-permute-start.4 = (bf16[4,48,1280]{2,1,0:T(8,128)(2,1)S(1)}, bf16[4,48,1280]{2,1,0:T(8,128)(2,1)}, u32[]{:S(2)}, u32[]{:S(2)}) collective-permute-start(bf16[4,48,1280]{2,1,0:T(8,128)(2,1)S(1)} %pad_maximum_fusion.1.refs_0_), channel_id=1, source_target_pairs={{0,1},{1,0},{2,3},{3,2},{4,5},{5,4},{6,7},{7,6},{8,9},{9,8},{10,11... | collective-permute-start | bytes 1474568 | tf_op jit(solution)/shard_map/ppermute | solution.py:57
  51.5 13.4 %collective-permute-start.11 = (bf16[4,48,1280]{2,1,0:T(8,128)(2,1)S(1)}, bf16[4,48,1280]{2,1,0:T(8,128)(2,1)}, u32[]{:S(2)}, u32[]{:S(2)}) collective-permute-start(bf16[4,48,1280]{2,1,0:T(8,128)(2,1)S(1)} %collective-permute-done.5.refs_1_), channel_id=1, source_target_pairs={{0,1},{1,0},{2,3},{3,2},{4,5},{5,4},{6,7},{7,6},{8,9},{9,8},{10,11... | collective-permute-start | bytes 1474568 | tf_op jit(solution)/shard_map/ppermute | solution.py:57
  53.0 25.1 %collective-permute-start.13 = (bf16[4,48,1280]{2,1,0:T(8,128)(2,1)}, bf16[4,48,1280]{2,1,0:T(8,128)(2,1)}, u32[]{:S(2)}, u32[]{:S(2)}) collective-permute-start(bf16[4,48,1280]{2,1,0:T(8,128)(2,1)} %collective-permute-done.4.refs_0_.refs_4_), channel_id=1, source_target_pairs={{0,2},{1,3},{2,0},{3,1},{4,6},{5,7},{6,4},{7,5},{8,10},{9,11},{10,... | collective-permute-start | bytes 1474568 | tf_op jit(solution)/shard_map/ppermute | solution.py:57
  53.0 25.1 %collective-permute-start.12 = (bf16[4,48,1920]{2,1,0:T(8,128)(2,1)S(1)}, bf16[4,48,1920]{2,1,0:T(8,128)(2,1)S(1)}, u32[]{:S(2)}, u32[]{:S(2)}) collective-permute-start(bf16[4,48,1920]{2,1,0:T(8,128)(2,1)S(1)} %pad_maximum_fusion.refs_0_), channel_id=1, source_target_pairs={{0,1},{1,0},{2,6},{3,7},{4,5},{5,4},{6,2},{7,3},{8,9},{9,8},{10,14... | collective-permute-start | bytes 2211848 | tf_op jit(solution)/shard_map/ppermute | solution.py:57
  64.9 13.2 %collective-permute-start.14 = (bf16[4,48,1280]{2,1,0:T(8,128)(2,1)}, bf16[4,48,1280]{2,1,0:T(8,128)(2,1)S(1)}, u32[]{:S(2)}, u32[]{:S(2)}) collective-permute-start(bf16[4,48,1280]{2,1,0:T(8,128)(2,1)} %collective-permute-done.11.refs_1_.refs_5_), channel_id=1, source_target_pairs={{0,2},{1,3},{2,0},{3,1},{4,6},{5,7},{6,4},{7,5},{8,10},{9,11},{10,... | collective-permute-start | bytes 1474568 | tf_op jit(solution)/shard_map/ppermute | solution.py:57
  64.9 241.7 %reduce-scatter.2.cloned.1.call-start = ((), (), s32[]{:S(2)}) async-start(), calls=%async_computation.1 | async-start | bytes 4866048 | tf_op jit(solution)/shard_map/reduce_scatter | solution.py:985
  65.2 23.0 %collective-permute-start.16 = (bf16[4,48,1920]{2,1,0:T(8,128)(2,1)S(1)}, bf16[4,48,1920]{2,1,0:T(8,128)(2,1)S(1)}, u32[]{:S(2)}, u32[]{:S(2)}) collective-permute-start(bf16[4,48,1920]{2,1,0:T(8,128)(2,1)S(1)} %pad_maximum_fusion.refs_0_), channel_id=1, source_target_pairs={{0,4},{1,5},{2,3},{3,2},{4,0},{5,1},{6,7},{7,6},{8,12},{9,13},{10,... | collective-permute-start | bytes 2211848 | tf_op jit(solution)/shard_map/ppermute | solution.py:57
  147.4 169.8 %all-gather.7.cloned.1.call-start = ((), (), s32[]{:S(2)}) async-start(), calls=%async_computation.3 | async-start | bytes 4718592 | tf_op jit(solution)/shard_map/all_gather | solution.py:1025
  147.5 48.4 %collective-permute-start.21 = (bf16[1024,768]{1,0:T(8,128)(2,1)}, bf16[1024,768]{1,0:T(8,128)(2,1)}, u32[]{:S(2)}, u32[]{:S(2)}) collective-permute-start(bf16[1024,768]{1,0:T(8,128)(2,1)} %get-tuple-element.129), channel_id=1, source_target_pairs={{0,1},{1,0},{2,3},{3,2},{4,5},{5,4},{6,7},{7,6},{8,9},{9,8},{10,11... | collective-permute-start | bytes 4718600 | tf_op jit(solution)/shard_map/ppermute | solution.py:61
  195.8 14.0 %collective-permute-start.22 = (bf16[2,2,4,48,2048]{4,3,2,1,0:T(8,128)(2,1)}, bf16[2,2,4,48,2048]{4,3,2,1,0:T(8,128)(2,1)S(1)}, u32[]{:S(2)}, u32[]{:S(2)}) collective-permute-start(bf16[2,2,4,48,2048]{4,3,2,1,0:T(8,128)(2,1)} %get-tuple-element.141), channel_id=1, source_target_pairs={{0,2},{1,3},{2,0},{3,1},{4,6},{5,7},{6,4},{7,5},{8,10},{9,11},{10,... | collective-permute-start | bytes 9437192 | tf_op jit(solution)/shard_map/ppermute | solution.py:57
  217.0 24.9 %collective-permute-start.23 = (bf16[2,4,48,2048]{3,2,1,0:T(8,128)(2,1)}, bf16[2,4,48,2048]{3,2,1,0:T(8,128)(2,1)}, u32[]{:S(2)}, u32[]{:S(2)}) collective-permute-start(bf16[2,4,48,2048]{3,2,1,0:T(8,128)(2,1)} %get-tuple-element.184), channel_id=1, source_target_pairs={{0,4},{1,5},{2,3},{3,2},{4,0},{5,1},{6,7},{7,6},{8,12},{9,13},{10,... | collective-permute-start | bytes 4718600 | tf_op jit(solution)/shard_map/ppermute | solution.py:57
  245.9 14.3 %collective-permute-start.26 = (bf16[4,1,48,1280]{3,2,1,0:T(8,128)(2,1)}, bf16[4,1,48,1280]{3,2,1,0:T(8,128)(2,1)S(1)}, u32[]{:S(2)}, u32[]{:S(2)}) collective-permute-start(bf16[4,1,48,1280]{3,2,1,0:T(8,128)(2,1)} %get-tuple-element.188), channel_id=1, source_target_pairs={{0,4},{1,5},{2,6},{3,7},{4,0},{5,1},{6,2},{7,3},{8,12},{9,13},{10,... | collective-permute-start | bytes 1474568 | tf_op jit(solution)/shard_map/ppermute | solution.py:57
  246.7 13.5 %collective-permute-start.25 = (bf16[4,48,2048]{2,1,0:T(8,128)(2,1)}, bf16[4,48,2048]{2,1,0:T(8,128)(2,1)S(1)}, u32[]{:S(2)}, u32[]{:S(2)}) collective-permute-start(bf16[4,48,2048]{2,1,0:T(8,128)(2,1)} %get-tuple-element.186), channel_id=1, source_target_pairs={{0,1},{1,0},{2,6},{3,7},{4,5},{5,4},{6,2},{7,3},{8,9},{9,8},{10,14... | collective-permute-start | bytes 2359304 | tf_op jit(solution)/shard_map/ppermute | solution.py:57
  261.1 17.4 %collective-permute-start.29 = (bf16[48,2048]{1,0:T(8,128)(2,1)}, bf16[48,2048]{1,0:T(8,128)(2,1)S(1)}, u32[]{:S(2)}, u32[]{:S(2)}) collective-permute-start(bf16[48,2048]{1,0:T(8,128)(2,1)} %get-tuple-element.190), channel_id=1, source_target_pairs={{0,24},{1,25},{2,26},{3,27},{4,28},{5,29},{6,30},{7,31},{8,0},{9,1... | collective-permute-start | bytes 589832 | tf_op jit(solution)/shard_map/ppermute | solution.py:57
  262.7 17.4 %collective-permute-start.28 = (bf16[48,2048]{1,0:T(8,128)(2,1)S(1)}, bf16[48,2048]{1,0:T(8,128)(2,1)S(1)}, u32[]{:S(2)}, u32[]{:S(2)}) collective-permute-start(bf16[48,2048]{1,0:T(8,128)(2,1)S(1)} %get-tuple-element.191), channel_id=1, source_target_pairs={{0,16},{1,17},{2,18},{3,19},{4,20},{5,21},{6,22},{7,23},{8,24},{9,... | collective-permute-start | bytes 589832 | tf_op jit(solution)/shard_map/ppermute | solution.py:57
  264.1 16.0 %collective-permute-start.27 = (bf16[48,2048]{1,0:T(8,128)(2,1)S(1)}, bf16[48,2048]{1,0:T(8,128)(2,1)S(1)}, u32[]{:S(2)}, u32[]{:S(2)}) collective-permute-start(bf16[48,2048]{1,0:T(8,128)(2,1)S(1)} %get-tuple-element.192), channel_id=1, source_target_pairs={{0,8},{1,9},{2,10},{3,11},{4,12},{5,13},{6,14},{7,15},{8,16},{9,17... | collective-permute-start | bytes 589832 | tf_op jit(solution)/shard_map/ppermute | solution.py:57
  266.3 23.6 %collective-permute-start.32 = (bf16[4,1,48,1280]{3,2,1,0:T(8,128)(2,1)S(1)}, bf16[4,1,48,1280]{3,2,1,0:T(8,128)(2,1)S(1)}, u32[]{:S(2)}, u32[]{:S(2)}) collective-permute-start(bf16[4,1,48,1280]{3,2,1,0:T(8,128)(2,1)S(1)} %fusion.2), channel_id=1, source_target_pairs={{0,1},{1,0},{2,3},{3,2},{4,5},{5,4},{6,7},{7,6},{8,9},{9,8},{10,11... | collective-permute-start | bytes 1474568 | tf_op jit(solution)/shard_map/ppermute | solution.py:57
  286.7 12.7 %collective-permute-start.31 = (bf16[4,1,48,1280]{3,2,1,0:T(8,128)(2,1)S(1)}, bf16[4,1,48,1280]{3,2,1,0:T(8,128)(2,1)S(1)}, u32[]{:S(2)}, u32[]{:S(2)}) collective-permute-start(bf16[4,1,48,1280]{3,2,1,0:T(8,128)(2,1)S(1)} %fusion.7), channel_id=1, source_target_pairs={{0,4},{1,5},{2,6},{3,7},{4,0},{5,1},{6,2},{7,3},{8,12},{9,13},{10,... | collective-permute-start | bytes 1474568 | tf_op jit(solution)/shard_map/ppermute | solution.py:57
  (30 other events, 268.7 us)
Sparse Core Ops, SparseCore 0:
  65.1 60.3 all-gather.4
  147.5 107.9 reduce-scatter.1
  259.8 53.5 all-gather.6
where the time goes:
time: 334 us; the launch traced here: 329 us
  Pallas kernels  173 us (52%)
  waiting for transfers between devices  57.3 us (17%)
  starting transfers between devices  44 us (13%)
  other arithmetic  23.7 us (7%)
  local copies, waits for them, and re-layouts  17.1 us (5%)
  between operations  14.3 us (4%)
    ppermute x34, waiting for transfers between devices, move(): return lax.ppermute(values, AXES, moves)  53 us
    ppermute x34, starting transfers between devices, move(): return lax.ppermute(values, AXES, moves)  40.6 us
    pallas_call x3, Pallas kernels, grads(): pl.pallas_call(functools.partial(grads_kernel, staged, rows, halves, widt...  35.4 us
    pallas_call x1, Pallas kernels, third_part(): pl.pallas_call(functools.partial(third_kernel, len(up_pieces), len(down_p...  26.3 us
    pallas_call x2, Pallas kernels, attn_bwd(): pl.pallas_call(attn_bwd_kernel, out_shape=(jax.ShapeDtypeStruct((seq, wid...  22.4 us
    pallas_call x1, Pallas kernels, second_part(): pl.pallas_call(functools.partial(second_kernel, staged, len(pieces)), out...  21.9 us
    pallas_call x1, Pallas kernels, first_part(): pl.pallas_call(functools.partial(first_kernel, len(pieces)), out_shape=(j...  20.1 us
    pallas_call x2, Pallas kernels, attn_fwd(): pl.pallas_call(attn_fwd_kernel, out_shape=(jax.ShapeDtypeStruct((seq, wid...  17.8 us
  transfers between devices with their start and end apart: 39, of which 17 were waited for; matrix products, arithmetic and copies ran while one was open for 8% of the time, Pallas kernels for 46%

commit v1 on v0

--- a/solution.py
+++ b/solution.py
@@ -982,7 +982,7 @@
 
     if staged:
         down_grad = down_grad.reshape(2 * dp_size, *shard_down.shape)
-        s_down = lax.psum_scatter(down_grad, AXES, scatter_dimension=0).astype(F32)
+        s_down = lax.psum_scatter(down_grad, AXES, scatter_dimension=0)
     else:
         s_down = plain_scatter(*down_grad)
     d_pre, normed_low, d_one, d_one_low, d_ctx, sums_one, sums_up = third_part(
@@ -1036,20 +1036,26 @@
         qs_got, qs_keep = core_stage(*own_parts)
         qs_keep, *up_parts = lax.optimization_barrier((qs_keep, *up_parts))
         qs_got, qs_keep = flip_stage(MOVE_Y, qs_got, qs_keep)
+        out_other, qs_keep, s_down = lax.optimization_barrier((out_other, qs_keep, s_down))
+        s_down = s_down.astype(F32)
+        out_whole = place(out_whole, out_other)
+        out_whole, qs_got = lax.optimization_barrier((out_whole, qs_got))
         s_up = z_sum(up_parts, up_keep)
         qs_parts, qs_keep = z_stage(qs_got, qs_keep, qo_in)
-        s_qkv = z_sum(qs_parts, qs_keep)[0]
-        in_both, s_qkv = lax.optimization_barrier((in_both, s_qkv))
+        in_both, qs_keep = lax.optimization_barrier((in_both, qs_keep))
         in_other = lax.dynamic_index_in_dim(in_both, 1 - mp_at, 0, keepdims=False)
         d_input = place(d_input, in_other)
+        d_input, qs_keep = lax.optimization_barrier((d_input, qs_keep))
+        s_qkv = z_sum(qs_parts, qs_keep)[0]
     else:
+        out_whole = place(out_whole, out_other)
         d_input = place(d_input, in_other)
         s_qkv = plain_scatter(own_parts[0][0], other_parts[0][0])
 
     cols = s_up[:, ff + width :].T
     g_w_qkv = s_qkv[:, : 3 * width].reshape(rows, pairs, 3, PAIR).transpose(0, 2, 1, 3)
     return (
-        place(out_whole, out_other),
+        out_whole,
         d_input,
         g_w_qkv.reshape(rows, 3, width),
         s_qkv[:, 3 * width].reshape(2, rows // 2),

time: 334 us -> 328 us (0.982)
  waiting for transfers between devices: 57.3 us -> 52.8 us
    ppermute x34, waiting for transfers between devices: 53 us -> 45 us  [move(): return lax.ppermute(values, AXES, moves)]
    all_gather x1, waiting for transfers between devices: 0.02 us -> 3.61 us  [body(): in_both = lax.all_gather(in_low, 'mp')]
  transfers between devices with their start and end apart: 39 -> 39, of which waited for: 17 -> 15; matrix products, arithmetic and copies ran while one was open for 8% -> 9% of each run, Pallas kernels for 46% -> 47%
where the time goes in v1:
time: 328 us; the launch traced here: 323 us
  Pallas kernels  172 us (52%)
  waiting for transfers between devices  52.8 us (16%)
  starting transfers between devices  43.6 us (13%)
  other arithmetic  23.9 us (7%)
  local copies, waits for them, and re-layouts  16.3 us (5%)
  between operations  14.3 us (4%)
    ppermute x34, waiting for transfers between devices, move(): return lax.ppermute(values, AXES, moves)  45 us
    ppermute x34, starting transfers between devices, move(): return lax.ppermute(values, AXES, moves)  40.3 us
    pallas_call x3, Pallas kernels, grads(): pl.pallas_call(functools.partial(grads_kernel, staged, rows, halves, widt...  35.2 us
    pallas_call x1, Pallas kernels, third_part(): pl.pallas_call(functools.partial(third_kernel, len(up_pieces), len(down_p...  26.3 us
    pallas_call x2, Pallas kernels, attn_bwd(): pl.pallas_call(attn_bwd_kernel, out_shape=(jax.ShapeDtypeStruct((seq, wid...  22.4 us
    pallas_call x1, Pallas kernels, second_part(): pl.pallas_call(functools.partial(second_kernel, staged, len(pieces)), out...  21.9 us
    pallas_call x1, Pallas kernels, first_part(): pl.pallas_call(functools.partial(first_kernel, len(pieces)), out_shape=(j...  20.1 us
    pallas_call x2, Pallas kernels, attn_fwd(): pl.pallas_call(attn_fwd_kernel, out_shape=(jax.ShapeDtypeStruct((seq, wid...  17.8 us
  transfers between devices with their start and end apart: 39, of which 15 were waited for; matrix products, arithmetic and copies ran while one was open for 9% of the time, Pallas kernels for 47%

profile of v1, /device:TPU:0, one launch (start us, length us, event | category | flops | bytes accessed | tf_op | source)
XLA Modules:
  0.0 323.4 jit_solution(12945281409454007829)
XLA Ops:
  10.8 4.1 %collective-permute-start.2 = (bf16[48,1280]{1,0:T(8,128)(2,1)S(1)}, bf16[48,1280]{1,0:T(8,128)(2,1)S(1)}, u32[]{:S(2)}, u32[]{:S(2)}) collective-permute-start(bf16[48,1280]{1,0:T(8,128)(2,1)S(1)} %get-tuple-element.214), channel_id=1, source_target_pairs={{0,16},{1,17},{2,18},{3,19},{4,20},{5,21},{6,22},{7,23},{8,24},{9,... | collective-permute-start | bytes 368648 | tf_op jit(solution)/shard_map/ppermute | solution.py:57
  18.8 5.7 %collective-permute-done.2 = bf16[48,1280]{1,0:T(8,128)(2,1)S(1)} collective-permute-done((bf16[48,1280]{1,0:T(8,128)(2,1)S(1)}, bf16[48,1280]{1,0:T(8,128)(2,1)S(1)}, u32[]{:S(2)}, u32[]{:S(2)}) %collective-permute-start.2) | collective-permute-done | bytes 122912 | tf_op jit(solution)/shard_map/ppermute | solution.py:57
  35.9 11.9 %collective-permute-done.7 = bf16[48,1920]{1,0:T(8,128)(2,1)S(1)} collective-permute-done((bf16[48,1920]{1,0:T(8,128)(2,1)S(1)}, bf16[48,1920]{1,0:T(8,128)(2,1)S(1)}, u32[]{:S(2)}, u32[]{:S(2)}) %collective-permute-start.7) | collective-permute-done | bytes 184352 | tf_op jit(solution)/shard_map/ppermute | solution.py:57
  55.4 8.7 %project.2 = (bf16[1024,1152]{1,0:T(8,128)(2,1)}, f32[8,768]{1,0:T(8,128)}, f32[1,1536]{1,0:T(1,128)}) custom-call(s32[4]{0:T(128)} %pad_add_fusion.1.where, bf16[2048,768]{1,0:T(8,128)(2,1)} %refs_0_.2, bf16[4,48,1280]{2,1,0:T(8,128)(2,1)} %copy-done.4, bf16[4,48,1280]{2,1,0:T(8,128)(2,1)} %copy-done.11, bf16[4,48,1280]{2,1,0:T(8,128)(2,1)} %copy-done.12, ...), custom_call_target="tpu_custom_call" | custom-call | flops 34800001024 | bytes 104400000 | tf_op jit(solution)/shard_map/project/pallas_call | solution.py:187
  65.8 8.9 %attn_fwd.2 = (bf16[1024,384]{1,0:T(8,128)(2,1)}, bf16[3,2,2,256,768]{4,3,2,1,0:T(8,128)(2,1)}) custom-call(s32[24]{0:T(128)} %get-tuple-element.216.table, bf16[1024,1152]{1,0:T(8,128)(2,1)} %get-tuple-element.110.qkv_ref), custom_call_target="tpu_custom_call" | custom-call | flops 2000000000 | bytes 6000000 | tf_op jit(solution)/shard_map/attn_fwd/pallas_call | solution.py:753
  74.7 3.4 %collective-permute-done.12.refs_1_ = bf16[4,48,1920]{2,1,0:T(8,128)(2,1)S(1)} collective-permute-done((bf16[4,48,1920]{2,1,0:T(8,128)(2,1)S(1)}, bf16[4,48,1920]{2,1,0:T(8,128)(2,1)S(1)}, u32[]{:S(2)}, u32[]{:S(2)}) %collective-permute-start.12) | collective-permute-done | bytes 737312 | tf_op jit(solution)/shard_map/ppermute | solution.py:57
  79.0 8.6 %project.3 = (bf16[1024,1152]{1,0:T(8,128)(2,1)}, f32[8,768]{1,0:T(8,128)}, f32[1,1536]{1,0:T(1,128)}) custom-call(s32[4]{0:T(128)} %pad_add_fusion.1.where, bf16[2048,768]{1,0:T(8,128)(2,1)} %refs_0_.2, bf16[4,48,1280]{2,1,0:T(8,128)(2,1)} %collective-permute-done.4.refs_0_.refs_4_, bf16[4,48,1280]{2,1,0:T(8,128)(2,1)} %collective-permute-done.11.refs_1_.refs_5_, ...), custom_call_target="tpu_custom_call" | custom-call | flops 34800001024 | bytes 104400000 | tf_op jit(solution)/shard_map/project/pallas_call | solution.py:187
  88.8 8.9 %attn_fwd.3 = (bf16[1024,384]{1,0:T(8,128)(2,1)}, bf16[3,2,2,256,768]{4,3,2,1,0:T(8,128)(2,1)}) custom-call(s32[24]{0:T(128)} %copy-done.14, bf16[1024,1152]{1,0:T(8,128)(2,1)} %get-tuple-element.120.qkv_ref), custom_call_target="tpu_custom_call" | custom-call | flops 2000000000 | bytes 6000000 | tf_op jit(solution)/shard_map/attn_fwd/pallas_call | solution.py:753
  102.0 20.1 %first_part.1 = (f32[1024,768]{1,0:T(8,128)}, f32[1024,128]{1,0:T(8,128)}, bf16[2,1024,1536]{2,1,0:T(8,128)(2,1)}, bf16[2,1024,1536]{2,1,0:T(8,128)(2,1)}) custom-call(s32[4]{0:T(128)} %pad_add_fusion.1.where, bf16[2048,768]{1,0:T(8,128)(2,1)} %refs_0_.2, bf16[1024,384]{1,0:T(8,128)(2,1)} %get-tuple-element.113.ctx0_ref.refs_4_, ...), custom_call_target="tpu_custom_call" | custom-call | flops 77599997952 | bytes 232800000 | tf_op jit(solution)/shard_map/first_part/pallas_call | solution.py:459
  122.1 3.4 %all-gather.5.cloned.1.call-done = bf16[1536,1536]{1,0:T(8,128)(2,1)} async-done(((bf16[48,1536]{1,0:T(8,128)(2,1)}), bf16[1536,1536]{1,0:T(8,128)(2,1)}) %all-gather.5.cloned.1.call-update) | async-done | bytes 4718608 | tf_op jit(solution)/shard_map/all_gather | solution.py:924
  125.5 21.9 %second_part.1 = (bf16[2048,768]{1,0:T(8,128)(2,1)}, bf16[1024,768]{1,0:T(8,128)(2,1)}, f32[1024,768]{1,0:T(8,128)}, f32[8,768]{1,0:T(8,128)}, bf16[16,2,48,1536]{3,2,1,0:T(8,128)(2,1)}) custom-call(s32[4]{0:T(128)} %pad_add_fusion.1.where, bf16[2,1024,1536]{2,1,0:T(8,128)(2,1)} %get-tuple-element.128.hid_ref, f32[1024,768]{1,0:T(8,128)} %get-tuple-element.129.z_ref, ...), custom_call_target="tpu_custom_call" | custom-call | flops 87199997952 | bytes 261600000 | tf_op jit(solution)/shard_map/second_part/pallas_call | solution.py:541
  149.0 26.3 %third_part.1 = (bf16[2,1024,1536]{2,1,0:T(8,128)(2,1)}, bf16[1024,768]{1,0:T(8,128)(2,1)}, f32[1024,768]{1,0:T(8,128)}, bf16[1024,768]{1,0:T(8,128)(2,1)}, bf16...) custom-call(s32[4]{0:T(128)} %pad_add_fusion.1.where, f32[1024,768]{1,0:T(8,128)} %get-tuple-element.132.d_ref, ...), custom_call_target="tpu_custom_call" | custom-call | flops 102400000000 | bytes 307200000 | tf_op jit(solution)/shard_map/third_part/pallas_call | solution.py:629
  175.3 20.4 %grads.3 = (bf16[2,2,4,48,2048]{4,3,2,1,0:T(8,128)(2,1)}, bf16[2,2,4,48,2048]{4,3,2,1,0:T(8,128)(2,1)}) custom-call(s32[4]{0:T(128)} %pad_add_fusion.1.where, bf16[1024,768]{1,0:T(8,128)(2,1)} %get-tuple-element.137.refs_0_, bf16[1024,768]{1,0:T(8,128)(2,1)} %get-tuple-element.138.refs_1_, bf16[2,1024,1536]{2,1,0:T(8,128)(2,1)} %get-tuple-element.139.refs_2_.refs_3_, ...), custom_call_target="tpu_custom_call" | custom-call | flops 80000000000 | bytes 240000000 | tf_op jit(solution)/shard_map/grads/pallas_call | solution.py:375
  195.8 11.3 %attn_bwd.2 = (bf16[1024,1152]{1,0:T(8,128)(2,1)}, f32[3,8,384]{2,1,0:T(8,128)}) custom-call(s32[24]{0:T(128)} %copy-done.14, bf16[1024,1152]{1,0:T(8,128)(2,1)} %get-tuple-element.120.qkv_ref, bf16[2,1024,384]{2,1,0:T(8,128)(2,1)} %get-tuple-element.155.d_ref, bf16[3,2,2,256,768]{4,3,2,1,0:T(8,128)(2,1)} %get-tuple-element.146.prob_ref), custom_call_target="tpu_custom_call" | custom-call | flops 45199998976 | bytes 135600000 | tf_op jit(solution)/shard_map/attn_bwd/pallas_call | solution.py:824
  208.8 5.6 %fusion.1 = (bf16[2,4,48,2048]{3,2,1,0:T(8,128)(2,1)}, bf16[2,4,48,2048]{3,2,1,0:T(8,128)(2,1)S(1)}) fusion(bf16[2,2,4,48,2048]{4,3,2,1,0:T(8,128)(2,1)} %copy-done, bf16[2,2,4,48,2048]{4,3,2,1,0:T(8,128)(2,1)} %get-tuple-element.150), kind=kLoop, calls=%fused_computation.4 | loop fusion | flops 6291456 | bytes 9437184 | tf_op jit(solution)/shard_map/convert_element_type | solution.py:673
  214.9 7.2 %grads.4 = (bf16[2,4,1,48,1280]{4,3,2,1,0:T(8,128)(2,1)}, bf16[2,4,1,48,1280]{4,3,2,1,0:T(8,128)(2,1)}) custom-call(s32[4]{0:T(128)} %pad_add_fusion.1.where, bf16[2048,768]{1,0:T(8,128)(2,1)} %refs_0_.2, bf16[1024,1152]{1,0:T(8,128)(2,1)} %get-tuple-element.152.refs_1_.other_ref, f32[3,8,384]{2,1,0:T(8,128)} %get-tuple-element.153.refs_2_), custom_call_target="tpu_custom_call" | custom-call | flops 28800000000 | bytes 86400000 | tf_op jit(solution)/shard_map/grads/pallas_call | solution.py:375
  222.2 11.1 %attn_bwd.3 = (bf16[1024,1152]{1,0:T(8,128)(2,1)}, f32[3,8,384]{2,1,0:T(8,128)}) custom-call(s32[24]{0:T(128)} %get-tuple-element.216.table, bf16[1024,1152]{1,0:T(8,128)(2,1)} %get-tuple-element.110.qkv_ref, bf16[2,1024,384]{2,1,0:T(8,128)(2,1)} %get-tuple-element.155.d_ref, bf16[3,2,2,256,768]{4,3,2,1,0:T(8,128)(2,1)} %get-tuple-element.156.prob_ref), custom_call_target="tpu_custom_call" | custom-call | flops 45199998976 | bytes 135600000 | tf_op jit(solution)/shard_map/attn_bwd/pallas_call | solution.py:824
  233.3 6.0 %collective-permute-done.23 = bf16[2,4,48,2048]{3,2,1,0:T(8,128)(2,1)} collective-permute-done((bf16[2,4,48,2048]{3,2,1,0:T(8,128)(2,1)}, bf16[2,4,48,2048]{3,2,1,0:T(8,128)(2,1)}, u32[]{:S(2)}, u32[]{:S(2)}) %collective-permute-start.23) | collective-permute-done | bytes 1572896 | tf_op jit(solution)/shard_map/ppermute | solution.py:57
  245.1 11.4 %last_part.1 = (f32[2048,768]{1,0:T(8,128)}, bf16[1024,768]{1,0:T(8,128)(2,1)}) custom-call(s32[4]{0:T(128)} %pad_add_fusion.1.where, bf16[1024,1152]{1,0:T(8,128)(2,1)} %get-tuple-element.164.own_ref.refs_1_, bf16[1024,1152]{1,0:T(8,128)(2,1)} %get-tuple-element.152.refs_1_.other_ref, f32[1024,768]{1,0:T(8,128)} %get-tuple-element.165.one_ref, ...), custom_call_target="tpu_custom_call" | custom-call | flops 48000000000 | bytes 144000000 | tf_op jit(solution)/shard_map/last_part/pallas_call | solution.py:236
  264.4 7.6 %grads.5 = (bf16[2,4,1,48,1280]{4,3,2,1,0:T(8,128)(2,1)}, bf16[2,4,1,48,1280]{4,3,2,1,0:T(8,128)(2,1)}) custom-call(s32[4]{0:T(128)} %pad_add_fusion.1.where, bf16[2048,768]{1,0:T(8,128)(2,1)} %refs_0_.2, bf16[1024,1152]{1,0:T(8,128)(2,1)} %get-tuple-element.164.own_ref.refs_1_, f32[3,8,384]{2,1,0:T(8,128)} %get-tuple-element.171.refs_2_), custom_call_target="tpu_custom_call" | custom-call | flops 28800000000 | bytes 86400000 | tf_op jit(solution)/shard_map/grads/pallas_call | solution.py:375
  272.0 4.4 %collective-permute-start.30 = (bf16[2,4,1,48,1280]{4,3,2,1,0:T(8,128)(2,1)}, bf16[2,4,1,48,1280]{4,3,2,1,0:T(8,128)(2,1)}, u32[]{:S(2)}, u32[]{:S(2)}) collective-permute-start(bf16[2,4,1,48,1280]{4,3,2,1,0:T(8,128)(2,1)} %get-tuple-element.174), channel_id=1, source_target_pairs={{0,2},{1,3},{2,0},{3,1},{4,6},{5,7},{6,4},{7,5},{8,10},{9,11},{10,... | collective-permute-start | bytes 2949128 | tf_op jit(solution)/shard_map/ppermute | solution.py:57
  289.2 9.1 %collective-permute-done.31 = bf16[4,1,48,1280]{3,2,0,1:T(8,128)(2,1)S(1)} collective-permute-done((bf16[4,1,48,1280]{3,2,0,1:T(8,128)(2,1)S(1)}, bf16[4,1,48,1280]{3,2,0,1:T(8,128)(2,1)S(1)}, u32[]{:S(2)}, u32[]{:S(2)}) %collective-permute-start.31) | collective-permute-done | bytes 491552 | tf_op jit(solution)/shard_map/ppermute | solution.py:57
  307.9 3.6 %all-gather.7.cloned.1.call-done = bf16[2048,768]{1,0:T(8,128)(2,1)} async-done(((bf16[1024,768]{1,0:T(8,128)(2,1)}), bf16[2048,768]{1,0:T(8,128)(2,1)}) %all-gather.7.cloned.1.call-update) | async-done | bytes 3145744 | tf_op jit(solution)/shard_map/all_gather | solution.py:1025
  311.5 3.3 %convert_dynamic-update-slice_fusion = f32[2048,768]{1,0:T(8,128)} fusion(f32[2048,768]{1,0:T(8,128)} %get-tuple-element.178, s32[]{:T(128)S(6)} %select_n.37, bf16[2,1024,768]{2,1,0:T(8,128)(2,1)} %bitcast.104, s32[]{:T(128)S(6)} %select_n.36), kind=kLoop, calls=%fused_computation | loop fusion | flops 786432 | bytes 4718600 | tf_op jit(solution)/shard_map/dynamic_update_slice | solution.py:970
  (143 shorter events, 76.1 us)
Async XLA Ops:
  7.2 118.3 %all-gather.5.cloned.1.call-start = ((), (), s32[]{:S(2)}) async-start(), calls=%async_computation.2 | async-start | bytes 4866048 | tf_op jit(solution)/shard_map/all_gather | solution.py:924
  10.8 13.6 %collective-permute-start.2 = (bf16[48,1280]{1,0:T(8,128)(2,1)S(1)}, bf16[48,1280]{1,0:T(8,128)(2,1)S(1)}, u32[]{:S(2)}, u32[]{:S(2)}) collective-permute-start(bf16[48,1280]{1,0:T(8,128)(2,1)S(1)} %get-tuple-element.214), channel_id=1, source_target_pairs={{0,16},{1,17},{2,18},{3,19},{4,20},{5,21},{6,22},{7,23},{8,24},{9,... | collective-permute-start | bytes 368648 | tf_op jit(solution)/shard_map/ppermute | solution.py:57
  25.2 22.7 %collective-permute-start.5 = (bf16[4,48,1280]{2,1,0:T(8,128)(2,1)S(1)}, bf16[4,48,1280]{2,1,0:T(8,128)(2,1)S(1)}, u32[]{:S(2)}, u32[]{:S(2)}) collective-permute-start(bf16[4,48,1280]{2,1,0:T(8,128)(2,1)S(1)} %pad_maximum_fusion.1.refs_0_), channel_id=1, source_target_pairs={{0,4},{1,5},{2,6},{3,7},{4,0},{5,1},{6,2},{7,3},{8,12},{9,13},{10,... | collective-permute-start | bytes 1474568 | tf_op jit(solution)/shard_map/ppermute | solution.py:57
  29.9 18.0 %collective-permute-start.7 = (bf16[48,1920]{1,0:T(8,128)(2,1)S(1)}, bf16[48,1920]{1,0:T(8,128)(2,1)S(1)}, u32[]{:S(2)}, u32[]{:S(2)}) collective-permute-start(bf16[48,1920]{1,0:T(8,128)(2,1)S(1)} %get-tuple-element.103), channel_id=1, source_target_pairs={{0,16},{1,17},{2,18},{3,19},{4,20},{5,21},{6,22},{7,23},{8,24},{9,... | collective-permute-start | bytes 552968 | tf_op jit(solution)/shard_map/ppermute | solution.py:57
  31.6 16.3 %collective-permute-start.6 = (bf16[48,1920]{1,0:T(8,128)(2,1)S(1)}, bf16[48,1920]{1,0:T(8,128)(2,1)S(1)}, u32[]{:S(2)}, u32[]{:S(2)}) collective-permute-start(bf16[48,1920]{1,0:T(8,128)(2,1)S(1)} %get-tuple-element.103), channel_id=1, source_target_pairs={{0,8},{1,9},{2,10},{3,11},{4,12},{5,13},{6,14},{7,15},{8,16},{9,17... | collective-permute-start | bytes 552968 | tf_op jit(solution)/shard_map/ppermute | solution.py:57
  33.5 21.1 %collective-permute-start.9 = (bf16[4,48,1280]{2,1,0:T(8,128)(2,1)S(1)}, bf16[4,48,1280]{2,1,0:T(8,128)(2,1)S(1)}, u32[]{:S(2)}, u32[]{:S(2)}) collective-permute-start(bf16[4,48,1280]{2,1,0:T(8,128)(2,1)S(1)} %pad_maximum_fusion.1.refs_0_), channel_id=1, source_target_pairs={{0,2},{1,3},{2,0},{3,1},{4,6},{5,7},{6,4},{7,5},{8,10},{9,11},{10,... | collective-permute-start | bytes 1474568 | tf_op jit(solution)/shard_map/ppermute | solution.py:57
  34.5 18.6 %collective-permute-start.4 = (bf16[4,48,1280]{2,1,0:T(8,128)(2,1)S(1)}, bf16[4,48,1280]{2,1,0:T(8,128)(2,1)}, u32[]{:S(2)}, u32[]{:S(2)}) collective-permute-start(bf16[4,48,1280]{2,1,0:T(8,128)(2,1)S(1)} %pad_maximum_fusion.1.refs_0_), channel_id=1, source_target_pairs={{0,1},{1,0},{2,3},{3,2},{4,5},{5,4},{6,7},{7,6},{8,9},{9,8},{10,11... | collective-permute-start | bytes 1474568 | tf_op jit(solution)/shard_map/ppermute | solution.py:57
  51.5 13.4 %collective-permute-start.11 = (bf16[4,48,1280]{2,1,0:T(8,128)(2,1)S(1)}, bf16[4,48,1280]{2,1,0:T(8,128)(2,1)}, u32[]{:S(2)}, u32[]{:S(2)}) collective-permute-start(bf16[4,48,1280]{2,1,0:T(8,128)(2,1)S(1)} %collective-permute-done.5.refs_1_), channel_id=1, source_target_pairs={{0,1},{1,0},{2,3},{3,2},{4,5},{5,4},{6,7},{7,6},{8,9},{9,8},{10,11... | collective-permute-start | bytes 1474568 | tf_op jit(solution)/shard_map/ppermute | solution.py:57
  53.0 25.1 %collective-permute-start.13 = (bf16[4,48,1280]{2,1,0:T(8,128)(2,1)}, bf16[4,48,1280]{2,1,0:T(8,128)(2,1)}, u32[]{:S(2)}, u32[]{:S(2)}) collective-permute-start(bf16[4,48,1280]{2,1,0:T(8,128)(2,1)} %collective-permute-done.4.refs_0_.refs_4_), channel_id=1, source_target_pairs={{0,2},{1,3},{2,0},{3,1},{4,6},{5,7},{6,4},{7,5},{8,10},{9,11},{10,... | collective-permute-start | bytes 1474568 | tf_op jit(solution)/shard_map/ppermute | solution.py:57
  53.0 25.1 %collective-permute-start.12 = (bf16[4,48,1920]{2,1,0:T(8,128)(2,1)S(1)}, bf16[4,48,1920]{2,1,0:T(8,128)(2,1)S(1)}, u32[]{:S(2)}, u32[]{:S(2)}) collective-permute-start(bf16[4,48,1920]{2,1,0:T(8,128)(2,1)S(1)} %pad_maximum_fusion.refs_0_), channel_id=1, source_target_pairs={{0,1},{1,0},{2,6},{3,7},{4,5},{5,4},{6,2},{7,3},{8,9},{9,8},{10,14... | collective-permute-start | bytes 2211848 | tf_op jit(solution)/shard_map/ppermute | solution.py:57
  64.9 13.2 %collective-permute-start.14 = (bf16[4,48,1280]{2,1,0:T(8,128)(2,1)}, bf16[4,48,1280]{2,1,0:T(8,128)(2,1)S(1)}, u32[]{:S(2)}, u32[]{:S(2)}) collective-permute-start(bf16[4,48,1280]{2,1,0:T(8,128)(2,1)} %collective-permute-done.11.refs_1_.refs_5_), channel_id=1, source_target_pairs={{0,2},{1,3},{2,0},{3,1},{4,6},{5,7},{6,4},{7,5},{8,10},{9,11},{10,... | collective-permute-start | bytes 1474568 | tf_op jit(solution)/shard_map/ppermute | solution.py:57
  64.9 219.3 %reduce-scatter.2.cloned.1.call-start = ((), (), s32[]{:S(2)}) async-start(), calls=%async_computation.1 | async-start | bytes 4866048 | tf_op jit(solution)/shard_map/reduce_scatter | solution.py:985
  65.2 23.0 %collective-permute-start.16 = (bf16[4,48,1920]{2,1,0:T(8,128)(2,1)S(1)}, bf16[4,48,1920]{2,1,0:T(8,128)(2,1)S(1)}, u32[]{:S(2)}, u32[]{:S(2)}) collective-permute-start(bf16[4,48,1920]{2,1,0:T(8,128)(2,1)S(1)} %pad_maximum_fusion.refs_0_), channel_id=1, source_target_pairs={{0,4},{1,5},{2,3},{3,2},{4,0},{5,1},{6,7},{7,6},{8,12},{9,13},{10,... | collective-permute-start | bytes 2211848 | tf_op jit(solution)/shard_map/ppermute | solution.py:57
  147.4 164.1 %all-gather.7.cloned.1.call-start = ((), (), s32[]{:S(2)}) async-start(), calls=%async_computation.3 | async-start | bytes 4718592 | tf_op jit(solution)/shard_map/all_gather | solution.py:1025
  147.5 48.4 %collective-permute-start.21 = (bf16[1024,768]{1,0:T(8,128)(2,1)}, bf16[1024,768]{1,0:T(8,128)(2,1)}, u32[]{:S(2)}, u32[]{:S(2)}) collective-permute-start(bf16[1024,768]{1,0:T(8,128)(2,1)} %get-tuple-element.136), channel_id=1, source_target_pairs={{0,1},{1,0},{2,3},{3,2},{4,5},{5,4},{6,7},{7,6},{8,9},{9,8},{10,11... | collective-permute-start | bytes 4718600 | tf_op jit(solution)/shard_map/ppermute | solution.py:61
  214.4 24.9 %collective-permute-start.23 = (bf16[2,4,48,2048]{3,2,1,0:T(8,128)(2,1)}, bf16[2,4,48,2048]{3,2,1,0:T(8,128)(2,1)}, u32[]{:S(2)}, u32[]{:S(2)}) collective-permute-start(bf16[2,4,48,2048]{3,2,1,0:T(8,128)(2,1)} %get-tuple-element.198), channel_id=1, source_target_pairs={{0,4},{1,5},{2,3},{3,2},{4,0},{5,1},{6,7},{7,6},{8,12},{9,13},{10,... | collective-permute-start | bytes 4718600 | tf_op jit(solution)/shard_map/ppermute | solution.py:57
  243.3 14.3 %collective-permute-start.26 = (bf16[4,1,48,1280]{3,2,1,0:T(8,128)(2,1)}, bf16[4,1,48,1280]{3,2,1,0:T(8,128)(2,1)S(1)}, u32[]{:S(2)}, u32[]{:S(2)}) collective-permute-start(bf16[4,1,48,1280]{3,2,1,0:T(8,128)(2,1)} %get-tuple-element.202), channel_id=1, source_target_pairs={{0,4},{1,5},{2,6},{3,7},{4,0},{5,1},{6,2},{7,3},{8,12},{9,13},{10,... | collective-permute-start | bytes 1474568 | tf_op jit(solution)/shard_map/ppermute | solution.py:57
  243.7 13.9 %collective-permute-start.25 = (bf16[4,48,2048]{2,1,0:T(8,128)(2,1)}, bf16[4,48,2048]{2,1,0:T(8,128)(2,1)S(1)}, u32[]{:S(2)}, u32[]{:S(2)}) collective-permute-start(bf16[4,48,2048]{2,1,0:T(8,128)(2,1)} %get-tuple-element.200), channel_id=1, source_target_pairs={{0,1},{1,0},{2,6},{3,7},{4,5},{5,4},{6,2},{7,3},{8,9},{9,8},{10,14... | collective-permute-start | bytes 2359304 | tf_op jit(solution)/shard_map/ppermute | solution.py:57
  258.5 17.9 %collective-permute-start.29 = (bf16[48,2048]{1,0:T(8,128)(2,1)}, bf16[48,2048]{1,0:T(8,128)(2,1)S(1)}, u32[]{:S(2)}, u32[]{:S(2)}) collective-permute-start(bf16[48,2048]{1,0:T(8,128)(2,1)} %get-tuple-element.204), channel_id=1, source_target_pairs={{0,24},{1,25},{2,26},{3,27},{4,28},{5,29},{6,30},{7,31},{8,0},{9,1... | collective-permute-start | bytes 589832 | tf_op jit(solution)/shard_map/ppermute | solution.py:57
  260.6 17.0 %collective-permute-start.28 = (bf16[48,2048]{1,0:T(8,128)(2,1)S(1)}, bf16[48,2048]{1,0:T(8,128)(2,1)S(1)}, u32[]{:S(2)}, u32[]{:S(2)}) collective-permute-start(bf16[48,2048]{1,0:T(8,128)(2,1)S(1)} %get-tuple-element.205), channel_id=1, source_target_pairs={{0,16},{1,17},{2,18},{3,19},{4,20},{5,21},{6,22},{7,23},{8,24},{9,... | collective-permute-start | bytes 589832 | tf_op jit(solution)/shard_map/ppermute | solution.py:57
  261.4 16.2 %collective-permute-start.27 = (bf16[48,2048]{1,0:T(8,128)(2,1)S(1)}, bf16[48,2048]{1,0:T(8,128)(2,1)S(1)}, u32[]{:S(2)}, u32[]{:S(2)}) collective-permute-start(bf16[48,2048]{1,0:T(8,128)(2,1)S(1)} %get-tuple-element.206), channel_id=1, source_target_pairs={{0,8},{1,9},{2,10},{3,11},{4,12},{5,13},{6,14},{7,15},{8,16},{9,17... | collective-permute-start | bytes 589832 | tf_op jit(solution)/shard_map/ppermute | solution.py:57
  263.4 34.9 %collective-permute-start.32 = (bf16[4,1,48,1280]{3,2,1,0:T(8,128)(2,1)S(1)}, bf16[4,1,48,1280]{3,2,1,0:T(8,128)(2,1)}, u32[]{:S(2)}, u32[]{:S(2)}) collective-permute-start(bf16[4,1,48,1280]{3,2,1,0:T(8,128)(2,1)S(1)} %fusion.2), channel_id=1, source_target_pairs={{0,1},{1,0},{2,3},{3,2},{4,5},{5,4},{6,7},{7,6},{8,9},{9,8},{10,11... | collective-permute-start | bytes 1474568 | tf_op jit(solution)/shard_map/ppermute | solution.py:57
  299.4 15.4 %collective-permute-start.33 = (bf16[1,48,1280]{2,1,0:T(8,128)(2,1)S(1)}, bf16[1,48,1280]{2,1,0:T(8,128)(2,1)S(1)}, u32[]{:S(2)}, u32[]{:S(2)}) collective-permute-start(bf16[1,48,1280]{2,1,0:T(8,128)(2,1)S(1)} %get-tuple-element.208), channel_id=1, source_target_pairs={{0,8},{1,9},{2,10},{3,11},{4,12},{5,13},{6,14},{7,15},{8,16},{9,17... | collective-permute-start | bytes 368648 | tf_op jit(solution)/shard_map/ppermute | solution.py:57
  302.0 12.9 %collective-permute-start.34 = (bf16[1,48,1280]{2,1,0:T(8,128)(2,1)S(1)}, bf16[1,48,1280]{2,1,0:T(8,128)(2,1)S(1)}, u32[]{:S(2)}, u32[]{:S(2)}) collective-permute-start(bf16[1,48,1280]{2,1,0:T(8,128)(2,1)S(1)} %get-tuple-element.209), channel_id=1, source_target_pairs={{0,16},{1,17},{2,18},{3,19},{4,20},{5,21},{6,22},{7,23},{8,24},{9,... | collective-permute-start | bytes 368648 | tf_op jit(solution)/shard_map/ppermute | solution.py:57
  (30 other events, 276.1 us)
Sparse Core Ops, SparseCore 0:
  65.1 60.3 all-gather.4
  147.5 107.6 reduce-scatter.1
  256.8 54.6 all-gather.6

commit v2 on v1

--- a/solution.py
+++ b/solution.py
@@ -176,10 +176,9 @@
         up_ref[...] = mm(turned, up[0], NN)[6:7] + mm(turned, up[1], NN)[7:8]
 
     tokens = tok_ref[...]
-    for at in range(0, span, 384):
-        proj_ref[:, at : at + 384] = (
-            mm(tokens, weights[0, :, at : at + 384], NN) + bias[0:1, at : at + 384]
-        ).astype(BF)
+    for at in range(0, span, 512):
+        end = min(at + 512, span)
+        proj_ref[:, at:end] = (mm(tokens, weights[0, :, at:end], NN) + bias[0:1, at:end]).astype(BF)
 
 
 def project(where, tokens, pieces, rows, seq, span, ff, tile=512):
@@ -318,9 +317,10 @@
             rhs = rhs_refs[n * halves + half]
             rhs = rhs.at[half] if len(rhs.shape) == 3 else rhs
             width = rhs.shape[1]
-            for at in range(0, width, 384):
-                result[half, :, first + at : first + at + 384] = mm(
-                    turned[n], rhs[:, at : at + 384], NN
+            for at in range(0, width, 512):
+                end = min(at + 512, width)
+                result[half, :, first + at : first + end] = mm(
+                    turned[n], rhs[:, at:end], NN
                 ).astype(BF)
             first += width
         if n_extra == 1:

time: 328 us -> 327 us (level)
  transfers between devices with their start and end apart: 39 -> 39, of which waited for: 15 -> 15; matrix products, arithmetic and copies ran while one was open for 9% -> 9% of each run, Pallas kernels for 47% -> 46%
where the time goes in v2:
time: 327 us; the launch traced here: 322 us
  Pallas kernels  169 us (52%)
  waiting for transfers between devices  55.5 us (17%)
  starting transfers between devices  43 us (13%)
  other arithmetic  24 us (7%)
  local copies, waits for them, and re-layouts  16.3 us (5%)
  between operations  14.3 us (4%)
    ppermute x34, waiting for transfers between devices, move(): return lax.ppermute(values, AXES, moves)  47 us
    ppermute x34, starting transfers between devices, move(): return lax.ppermute(values, AXES, moves)  39.7 us
    pallas_call x3, Pallas kernels, grads(): pl.pallas_call(functools.partial(grads_kernel, staged, rows, halves, widt...  32.6 us
    pallas_call x1, Pallas kernels, third_part(): pl.pallas_call(functools.partial(third_kernel, len(up_pieces), len(down_p...  25.9 us
    pallas_call x2, Pallas kernels, attn_bwd(): pl.pallas_call(attn_bwd_kernel, out_shape=(jax.ShapeDtypeStruct((seq, wid...  22.7 us
    pallas_call x1, Pallas kernels, second_part(): pl.pallas_call(functools.partial(second_kernel, staged, len(pieces)), out...  22.1 us
    pallas_call x1, Pallas kernels, first_part(): pl.pallas_call(functools.partial(first_kernel, len(pieces)), out_shape=(j...  20.2 us
    pallas_call x2, Pallas kernels, attn_fwd(): pl.pallas_call(attn_fwd_kernel, out_shape=(jax.ShapeDtypeStruct((seq, wid...  17.8 us
  transfers between devices with their start and end apart: 39, of which 15 were waited for; matrix products, arithmetic and copies ran while one was open for 9% of the time, Pallas kernels for 46%

profile of v2, /device:TPU:0, one launch (start us, length us, event | category | flops | bytes accessed | tf_op | source)
XLA Modules:
  0.0 322.3 jit_solution(5793466766658194035)
XLA Ops:
  10.8 4.1 %collective-permute-start.2 = (bf16[48,1280]{1,0:T(8,128)(2,1)S(1)}, bf16[48,1280]{1,0:T(8,128)(2,1)S(1)}, u32[]{:S(2)}, u32[]{:S(2)}) collective-permute-start(bf16[48,1280]{1,0:T(8,128)(2,1)S(1)} %get-tuple-element.214), channel_id=1, source_target_pairs={{0,16},{1,17},{2,18},{3,19},{4,20},{5,21},{6,22},{7,23},{8,24},{9,... | collective-permute-start | bytes 368648 | tf_op jit(solution)/shard_map/ppermute | solution.py:57
  18.8 5.7 %collective-permute-done.2 = bf16[48,1280]{1,0:T(8,128)(2,1)S(1)} collective-permute-done((bf16[48,1280]{1,0:T(8,128)(2,1)S(1)}, bf16[48,1280]{1,0:T(8,128)(2,1)S(1)}, u32[]{:S(2)}, u32[]{:S(2)}) %collective-permute-start.2) | collective-permute-done | bytes 122912 | tf_op jit(solution)/shard_map/ppermute | solution.py:57
  35.9 11.9 %collective-permute-done.7 = bf16[48,1920]{1,0:T(8,128)(2,1)S(1)} collective-permute-done((bf16[48,1920]{1,0:T(8,128)(2,1)S(1)}, bf16[48,1920]{1,0:T(8,128)(2,1)S(1)}, u32[]{:S(2)}, u32[]{:S(2)}) %collective-permute-start.7) | collective-permute-done | bytes 184352 | tf_op jit(solution)/shard_map/ppermute | solution.py:57
  55.4 8.3 %project.2 = (bf16[1024,1152]{1,0:T(8,128)(2,1)}, f32[8,768]{1,0:T(8,128)}, f32[1,1536]{1,0:T(1,128)}) custom-call(s32[4]{0:T(128)} %pad_add_fusion.1.where, bf16[2048,768]{1,0:T(8,128)(2,1)} %refs_0_.2, bf16[4,48,1280]{2,1,0:T(8,128)(2,1)} %copy-done.4, bf16[4,48,1280]{2,1,0:T(8,128)(2,1)} %copy-done.11, bf16[4,48,1280]{2,1,0:T(8,128)(2,1)} %copy-done.12, ...), custom_call_target="tpu_custom_call" | custom-call | flops 34800001024 | bytes 104400000 | tf_op jit(solution)/shard_map/project/pallas_call | solution.py:186
  65.8 8.9 %attn_fwd.2 = (bf16[1024,384]{1,0:T(8,128)(2,1)}, bf16[3,2,2,256,768]{4,3,2,1,0:T(8,128)(2,1)}) custom-call(s32[24]{0:T(128)} %get-tuple-element.216.table, bf16[1024,1152]{1,0:T(8,128)(2,1)} %get-tuple-element.110.qkv_ref), custom_call_target="tpu_custom_call" | custom-call | flops 2000000000 | bytes 6000000 | tf_op jit(solution)/shard_map/attn_fwd/pallas_call | solution.py:753
  74.7 3.4 %collective-permute-done.12.refs_1_ = bf16[4,48,1920]{2,1,0:T(8,128)(2,1)S(1)} collective-permute-done((bf16[4,48,1920]{2,1,0:T(8,128)(2,1)S(1)}, bf16[4,48,1920]{2,1,0:T(8,128)(2,1)S(1)}, u32[]{:S(2)}, u32[]{:S(2)}) %collective-permute-start.12) | collective-permute-done | bytes 737312 | tf_op jit(solution)/shard_map/ppermute | solution.py:57
  79.0 8.2 %project.3 = (bf16[1024,1152]{1,0:T(8,128)(2,1)}, f32[8,768]{1,0:T(8,128)}, f32[1,1536]{1,0:T(1,128)}) custom-call(s32[4]{0:T(128)} %pad_add_fusion.1.where, bf16[2048,768]{1,0:T(8,128)(2,1)} %refs_0_.2, bf16[4,48,1280]{2,1,0:T(8,128)(2,1)} %collective-permute-done.4.refs_0_.refs_4_, bf16[4,48,1280]{2,1,0:T(8,128)(2,1)} %collective-permute-done.11.refs_1_.refs_5_, ...), custom_call_target="tpu_custom_call" | custom-call | flops 34800001024 | bytes 104400000 | tf_op jit(solution)/shard_map/project/pallas_call | solution.py:186
  88.4 8.9 %attn_fwd.3 = (bf16[1024,384]{1,0:T(8,128)(2,1)}, bf16[3,2,2,256,768]{4,3,2,1,0:T(8,128)(2,1)}) custom-call(s32[24]{0:T(128)} %copy-done.14, bf16[1024,1152]{1,0:T(8,128)(2,1)} %get-tuple-element.120.qkv_ref), custom_call_target="tpu_custom_call" | custom-call | flops 2000000000 | bytes 6000000 | tf_op jit(solution)/shard_map/attn_fwd/pallas_call | solution.py:753
  101.8 20.2 %first_part.1 = (f32[1024,768]{1,0:T(8,128)}, f32[1024,128]{1,0:T(8,128)}, bf16[2,1024,1536]{2,1,0:T(8,128)(2,1)}, bf16[2,1024,1536]{2,1,0:T(8,128)(2,1)}) custom-call(s32[4]{0:T(128)} %pad_add_fusion.1.where, bf16[2048,768]{1,0:T(8,128)(2,1)} %refs_0_.2, bf16[1024,384]{1,0:T(8,128)(2,1)} %get-tuple-element.113.ctx0_ref.refs_4_, ...), custom_call_target="tpu_custom_call" | custom-call | flops 77599997952 | bytes 232800000 | tf_op jit(solution)/shard_map/first_part/pallas_call | solution.py:459
  121.9 3.3 %all-gather.5.cloned.1.call-done = bf16[1536,1536]{1,0:T(8,128)(2,1)} async-done(((bf16[48,1536]{1,0:T(8,128)(2,1)}), bf16[1536,1536]{1,0:T(8,128)(2,1)}) %all-gather.5.cloned.1.call-update) | async-done | bytes 4718608 | tf_op jit(solution)/shard_map/all_gather | solution.py:924
  125.3 22.1 %second_part.1 = (bf16[2048,768]{1,0:T(8,128)(2,1)}, bf16[1024,768]{1,0:T(8,128)(2,1)}, f32[1024,768]{1,0:T(8,128)}, f32[8,768]{1,0:T(8,128)}, bf16[16,2,48,1536]{3,2,1,0:T(8,128)(2,1)}) custom-call(s32[4]{0:T(128)} %pad_add_fusion.1.where, bf16[2,1024,1536]{2,1,0:T(8,128)(2,1)} %get-tuple-element.128.hid_ref, f32[1024,768]{1,0:T(8,128)} %get-tuple-element.129.z_ref, ...), custom_call_target="tpu_custom_call" | custom-call | flops 87199997952 | bytes 261600000 | tf_op jit(solution)/shard_map/second_part/pallas_call | solution.py:541
  149.0 25.9 %third_part.1 = (bf16[2,1024,1536]{2,1,0:T(8,128)(2,1)}, bf16[1024,768]{1,0:T(8,128)(2,1)}, f32[1024,768]{1,0:T(8,128)}, bf16[1024,768]{1,0:T(8,128)(2,1)}, bf16...) custom-call(s32[4]{0:T(128)} %pad_add_fusion.1.where, f32[1024,768]{1,0:T(8,128)} %get-tuple-element.132.d_ref, ...), custom_call_target="tpu_custom_call" | custom-call | flops 102400000000 | bytes 307200000 | tf_op jit(solution)/shard_map/third_part/pallas_call | solution.py:629
  174.9 18.7 %grads.3 = (bf16[2,2,4,48,2048]{4,3,2,1,0:T(8,128)(2,1)}, bf16[2,2,4,48,2048]{4,3,2,1,0:T(8,128)(2,1)}) custom-call(s32[4]{0:T(128)} %pad_add_fusion.1.where, bf16[1024,768]{1,0:T(8,128)(2,1)} %get-tuple-element.137.refs_0_, bf16[1024,768]{1,0:T(8,128)(2,1)} %get-tuple-element.138.refs_1_, bf16[2,1024,1536]{2,1,0:T(8,128)(2,1)} %get-tuple-element.139.refs_2_.refs_3_, ...), custom_call_target="tpu_custom_call" | custom-call | flops 80000000000 | bytes 240000000 | tf_op jit(solution)/shard_map/grads/pallas_call | solution.py:375
  193.7 11.6 %attn_bwd.2 = (bf16[1024,1152]{1,0:T(8,128)(2,1)}, f32[3,8,384]{2,1,0:T(8,128)}) custom-call(s32[24]{0:T(128)} %copy-done.14, bf16[1024,1152]{1,0:T(8,128)(2,1)} %get-tuple-element.120.qkv_ref, bf16[2,1024,384]{2,1,0:T(8,128)(2,1)} %get-tuple-element.155.d_ref, bf16[3,2,2,256,768]{4,3,2,1,0:T(8,128)(2,1)} %get-tuple-element.146.prob_ref), custom_call_target="tpu_custom_call" | custom-call | flops 45199998976 | bytes 135600000 | tf_op jit(solution)/shard_map/attn_bwd/pallas_call | solution.py:824
  206.9 5.7 %fusion.1 = (bf16[2,4,48,2048]{3,2,1,0:T(8,128)(2,1)}, bf16[2,4,48,2048]{3,2,1,0:T(8,128)(2,1)S(1)}) fusion(bf16[2,2,4,48,2048]{4,3,2,1,0:T(8,128)(2,1)} %copy-done, bf16[2,2,4,48,2048]{4,3,2,1,0:T(8,128)(2,1)} %get-tuple-element.150), kind=kLoop, calls=%fused_computation.4 | loop fusion | flops 6291456 | bytes 9437184 | tf_op jit(solution)/shard_map/convert_element_type | solution.py:673
  212.8 6.8 %grads.4 = (bf16[2,4,1,48,1280]{4,3,2,1,0:T(8,128)(2,1)}, bf16[2,4,1,48,1280]{4,3,2,1,0:T(8,128)(2,1)}) custom-call(s32[4]{0:T(128)} %pad_add_fusion.1.where, bf16[2048,768]{1,0:T(8,128)(2,1)} %refs_0_.2, bf16[1024,1152]{1,0:T(8,128)(2,1)} %get-tuple-element.152.refs_1_.other_ref, f32[3,8,384]{2,1,0:T(8,128)} %get-tuple-element.153.refs_2_), custom_call_target="tpu_custom_call" | custom-call | flops 28800000000 | bytes 86400000 | tf_op jit(solution)/shard_map/grads/pallas_call | solution.py:375
  220.2 11.1 %attn_bwd.3 = (bf16[1024,1152]{1,0:T(8,128)(2,1)}, f32[3,8,384]{2,1,0:T(8,128)}) custom-call(s32[24]{0:T(128)} %get-tuple-element.216.table, bf16[1024,1152]{1,0:T(8,128)(2,1)} %get-tuple-element.110.qkv_ref, bf16[2,1024,384]{2,1,0:T(8,128)(2,1)} %get-tuple-element.155.d_ref, bf16[3,2,2,256,768]{4,3,2,1,0:T(8,128)(2,1)} %get-tuple-element.156.prob_ref), custom_call_target="tpu_custom_call" | custom-call | flops 45199998976 | bytes 135600000 | tf_op jit(solution)/shard_map/attn_bwd/pallas_call | solution.py:824
  231.3 6.2 %collective-permute-done.23 = bf16[2,4,48,2048]{3,2,1,0:T(8,128)(2,1)} collective-permute-done((bf16[2,4,48,2048]{3,2,1,0:T(8,128)(2,1)}, bf16[2,4,48,2048]{3,2,1,0:T(8,128)(2,1)}, u32[]{:S(2)}, u32[]{:S(2)}) %collective-permute-start.23) | collective-permute-done | bytes 1572896 | tf_op jit(solution)/shard_map/ppermute | solution.py:57
  243.1 11.4 %last_part.1 = (f32[2048,768]{1,0:T(8,128)}, bf16[1024,768]{1,0:T(8,128)(2,1)}) custom-call(s32[4]{0:T(128)} %pad_add_fusion.1.where, bf16[1024,1152]{1,0:T(8,128)(2,1)} %get-tuple-element.164.own_ref.refs_1_, bf16[1024,1152]{1,0:T(8,128)(2,1)} %get-tuple-element.152.refs_1_.other_ref, f32[1024,768]{1,0:T(8,128)} %get-tuple-element.165.one_ref, ...), custom_call_target="tpu_custom_call" | custom-call | flops 48000000000 | bytes 144000000 | tf_op jit(solution)/shard_map/last_part/pallas_call | solution.py:235
  262.8 7.2 %grads.5 = (bf16[2,4,1,48,1280]{4,3,2,1,0:T(8,128)(2,1)}, bf16[2,4,1,48,1280]{4,3,2,1,0:T(8,128)(2,1)}) custom-call(s32[4]{0:T(128)} %pad_add_fusion.1.where, bf16[2048,768]{1,0:T(8,128)(2,1)} %refs_0_.2, bf16[1024,1152]{1,0:T(8,128)(2,1)} %get-tuple-element.164.own_ref.refs_1_, f32[3,8,384]{2,1,0:T(8,128)} %get-tuple-element.171.refs_2_), custom_call_target="tpu_custom_call" | custom-call | flops 28800000000 | bytes 86400000 | tf_op jit(solution)/shard_map/grads/pallas_call | solution.py:375
  269.9 4.1 %collective-permute-start.30 = (bf16[2,4,1,48,1280]{4,3,2,1,0:T(8,128)(2,1)}, bf16[2,4,1,48,1280]{4,3,2,1,0:T(8,128)(2,1)}, u32[]{:S(2)}, u32[]{:S(2)}) collective-permute-start(bf16[2,4,1,48,1280]{4,3,2,1,0:T(8,128)(2,1)} %get-tuple-element.174), channel_id=1, source_target_pairs={{0,2},{1,3},{2,0},{3,1},{4,6},{5,7},{6,4},{7,5},{8,10},{9,11},{10,... | collective-permute-start | bytes 2949128 | tf_op jit(solution)/shard_map/ppermute | solution.py:57
  287.4 9.1 %collective-permute-done.31 = bf16[4,1,48,1280]{3,2,0,1:T(8,128)(2,1)S(1)} collective-permute-done((bf16[4,1,48,1280]{3,2,0,1:T(8,128)(2,1)S(1)}, bf16[4,1,48,1280]{3,2,0,1:T(8,128)(2,1)S(1)}, u32[]{:S(2)}, u32[]{:S(2)}) %collective-permute-start.31) | collective-permute-done | bytes 491552 | tf_op jit(solution)/shard_map/ppermute | solution.py:57
  306.1 4.3 %all-gather.7.cloned.1.call-done = bf16[2048,768]{1,0:T(8,128)(2,1)} async-done(((bf16[1024,768]{1,0:T(8,128)(2,1)}), bf16[2048,768]{1,0:T(8,128)(2,1)}) %all-gather.7.cloned.1.call-update) | async-done | bytes 3145744 | tf_op jit(solution)/shard_map/all_gather | solution.py:1025
  310.4 3.3 %convert_dynamic-update-slice_fusion = f32[2048,768]{1,0:T(8,128)} fusion(f32[2048,768]{1,0:T(8,128)} %get-tuple-element.178, s32[]{:T(128)S(6)} %select_n.37, bf16[2,1024,768]{2,1,0:T(8,128)(2,1)} %bitcast.104, s32[]{:T(128)S(6)} %select_n.36), kind=kLoop, calls=%fused_computation | loop fusion | flops 786432 | bytes 4718600 | tf_op jit(solution)/shard_map/dynamic_update_slice | solution.py:970
  (143 shorter events, 77.7 us)
Async XLA Ops:
  7.2 118.1 %all-gather.5.cloned.1.call-start = ((), (), s32[]{:S(2)}) async-start(), calls=%async_computation.2 | async-start | bytes 4866048 | tf_op jit(solution)/shard_map/all_gather | solution.py:924
  10.8 13.6 %collective-permute-start.2 = (bf16[48,1280]{1,0:T(8,128)(2,1)S(1)}, bf16[48,1280]{1,0:T(8,128)(2,1)S(1)}, u32[]{:S(2)}, u32[]{:S(2)}) collective-permute-start(bf16[48,1280]{1,0:T(8,128)(2,1)S(1)} %get-tuple-element.214), channel_id=1, source_target_pairs={{0,16},{1,17},{2,18},{3,19},{4,20},{5,21},{6,22},{7,23},{8,24},{9,... | collective-permute-start | bytes 368648 | tf_op jit(solution)/shard_map/ppermute | solution.py:57
  25.2 22.7 %collective-permute-start.5 = (bf16[4,48,1280]{2,1,0:T(8,128)(2,1)S(1)}, bf16[4,48,1280]{2,1,0:T(8,128)(2,1)S(1)}, u32[]{:S(2)}, u32[]{:S(2)}) collective-permute-start(bf16[4,48,1280]{2,1,0:T(8,128)(2,1)S(1)} %pad_maximum_fusion.1.refs_0_), channel_id=1, source_target_pairs={{0,4},{1,5},{2,6},{3,7},{4,0},{5,1},{6,2},{7,3},{8,12},{9,13},{10,... | collective-permute-start | bytes 1474568 | tf_op jit(solution)/shard_map/ppermute | solution.py:57
  29.9 18.0 %collective-permute-start.7 = (bf16[48,1920]{1,0:T(8,128)(2,1)S(1)}, bf16[48,1920]{1,0:T(8,128)(2,1)S(1)}, u32[]{:S(2)}, u32[]{:S(2)}) collective-permute-start(bf16[48,1920]{1,0:T(8,128)(2,1)S(1)} %get-tuple-element.103), channel_id=1, source_target_pairs={{0,16},{1,17},{2,18},{3,19},{4,20},{5,21},{6,22},{7,23},{8,24},{9,... | collective-permute-start | bytes 552968 | tf_op jit(solution)/shard_map/ppermute | solution.py:57
  31.6 16.3 %collective-permute-start.6 = (bf16[48,1920]{1,0:T(8,128)(2,1)S(1)}, bf16[48,1920]{1,0:T(8,128)(2,1)S(1)}, u32[]{:S(2)}, u32[]{:S(2)}) collective-permute-start(bf16[48,1920]{1,0:T(8,128)(2,1)S(1)} %get-tuple-element.103), channel_id=1, source_target_pairs={{0,8},{1,9},{2,10},{3,11},{4,12},{5,13},{6,14},{7,15},{8,16},{9,17... | collective-permute-start | bytes 552968 | tf_op jit(solution)/shard_map/ppermute | solution.py:57
  33.5 21.1 %collective-permute-start.9 = (bf16[4,48,1280]{2,1,0:T(8,128)(2,1)S(1)}, bf16[4,48,1280]{2,1,0:T(8,128)(2,1)S(1)}, u32[]{:S(2)}, u32[]{:S(2)}) collective-permute-start(bf16[4,48,1280]{2,1,0:T(8,128)(2,1)S(1)} %pad_maximum_fusion.1.refs_0_), channel_id=1, source_target_pairs={{0,2},{1,3},{2,0},{3,1},{4,6},{5,7},{6,4},{7,5},{8,10},{9,11},{10,... | collective-permute-start | bytes 1474568 | tf_op jit(solution)/shard_map/ppermute | solution.py:57
  34.5 18.6 %collective-permute-start.4 = (bf16[4,48,1280]{2,1,0:T(8,128)(2,1)S(1)}, bf16[4,48,1280]{2,1,0:T(8,128)(2,1)}, u32[]{:S(2)}, u32[]{:S(2)}) collective-permute-start(bf16[4,48,1280]{2,1,0:T(8,128)(2,1)S(1)} %pad_maximum_fusion.1.refs_0_), channel_id=1, source_target_pairs={{0,1},{1,0},{2,3},{3,2},{4,5},{5,4},{6,7},{7,6},{8,9},{9,8},{10,11... | collective-permute-start | bytes 1474568 | tf_op jit(solution)/shard_map/ppermute | solution.py:57
  51.5 13.4 %collective-permute-start.11 = (bf16[4,48,1280]{2,1,0:T(8,128)(2,1)S(1)}, bf16[4,48,1280]{2,1,0:T(8,128)(2,1)}, u32[]{:S(2)}, u32[]{:S(2)}) collective-permute-start(bf16[4,48,1280]{2,1,0:T(8,128)(2,1)S(1)} %collective-permute-done.5.refs_1_), channel_id=1, source_target_pairs={{0,1},{1,0},{2,3},{3,2},{4,5},{5,4},{6,7},{7,6},{8,9},{9,8},{10,11... | collective-permute-start | bytes 1474568 | tf_op jit(solution)/shard_map/ppermute | solution.py:57
  53.0 25.1 %collective-permute-start.13 = (bf16[4,48,1280]{2,1,0:T(8,128)(2,1)}, bf16[4,48,1280]{2,1,0:T(8,128)(2,1)}, u32[]{:S(2)}, u32[]{:S(2)}) collective-permute-start(bf16[4,48,1280]{2,1,0:T(8,128)(2,1)} %collective-permute-done.4.refs_0_.refs_4_), channel_id=1, source_target_pairs={{0,2},{1,3},{2,0},{3,1},{4,6},{5,7},{6,4},{7,5},{8,10},{9,11},{10,... | collective-permute-start | bytes 1474568 | tf_op jit(solution)/shard_map/ppermute | solution.py:57
  53.0 25.0 %collective-permute-start.12 = (bf16[4,48,1920]{2,1,0:T(8,128)(2,1)S(1)}, bf16[4,48,1920]{2,1,0:T(8,128)(2,1)S(1)}, u32[]{:S(2)}, u32[]{:S(2)}) collective-permute-start(bf16[4,48,1920]{2,1,0:T(8,128)(2,1)S(1)} %pad_maximum_fusion.refs_0_), channel_id=1, source_target_pairs={{0,1},{1,0},{2,6},{3,7},{4,5},{5,4},{6,2},{7,3},{8,9},{9,8},{10,14... | collective-permute-start | bytes 2211848 | tf_op jit(solution)/shard_map/ppermute | solution.py:57
  64.9 13.2 %collective-permute-start.14 = (bf16[4,48,1280]{2,1,0:T(8,128)(2,1)}, bf16[4,48,1280]{2,1,0:T(8,128)(2,1)S(1)}, u32[]{:S(2)}, u32[]{:S(2)}) collective-permute-start(bf16[4,48,1280]{2,1,0:T(8,128)(2,1)} %collective-permute-done.11.refs_1_.refs_5_), channel_id=1, source_target_pairs={{0,2},{1,3},{2,0},{3,1},{4,6},{5,7},{6,4},{7,5},{8,10},{9,11},{10,... | collective-permute-start | bytes 1474568 | tf_op jit(solution)/shard_map/ppermute | solution.py:57
  64.9 217.7 %reduce-scatter.2.cloned.1.call-start = ((), (), s32[]{:S(2)}) async-start(), calls=%async_computation.1 | async-start | bytes 4866048 | tf_op jit(solution)/shard_map/reduce_scatter | solution.py:985
  65.2 22.6 %collective-permute-start.16 = (bf16[4,48,1920]{2,1,0:T(8,128)(2,1)S(1)}, bf16[4,48,1920]{2,1,0:T(8,128)(2,1)S(1)}, u32[]{:S(2)}, u32[]{:S(2)}) collective-permute-start(bf16[4,48,1920]{2,1,0:T(8,128)(2,1)S(1)} %pad_maximum_fusion.refs_0_), channel_id=1, source_target_pairs={{0,4},{1,5},{2,3},{3,2},{4,0},{5,1},{6,7},{7,6},{8,12},{9,13},{10,... | collective-permute-start | bytes 2211848 | tf_op jit(solution)/shard_map/ppermute | solution.py:57
  147.4 163.0 %all-gather.7.cloned.1.call-start = ((), (), s32[]{:S(2)}) async-start(), calls=%async_computation.3 | async-start | bytes 4718592 | tf_op jit(solution)/shard_map/all_gather | solution.py:1025
  147.5 46.2 %collective-permute-start.21 = (bf16[1024,768]{1,0:T(8,128)(2,1)}, bf16[1024,768]{1,0:T(8,128)(2,1)}, u32[]{:S(2)}, u32[]{:S(2)}) collective-permute-start(bf16[1024,768]{1,0:T(8,128)(2,1)} %get-tuple-element.136), channel_id=1, source_target_pairs={{0,1},{1,0},{2,3},{3,2},{4,5},{5,4},{6,7},{7,6},{8,9},{9,8},{10,11... | collective-permute-start | bytes 4718600 | tf_op jit(solution)/shard_map/ppermute | solution.py:61
  212.6 24.9 %collective-permute-start.23 = (bf16[2,4,48,2048]{3,2,1,0:T(8,128)(2,1)}, bf16[2,4,48,2048]{3,2,1,0:T(8,128)(2,1)}, u32[]{:S(2)}, u32[]{:S(2)}) collective-permute-start(bf16[2,4,48,2048]{3,2,1,0:T(8,128)(2,1)} %get-tuple-element.198), channel_id=1, source_target_pairs={{0,4},{1,5},{2,3},{3,2},{4,0},{5,1},{6,7},{7,6},{8,12},{9,13},{10,... | collective-permute-start | bytes 4718600 | tf_op jit(solution)/shard_map/ppermute | solution.py:57
  241.4 14.5 %collective-permute-start.26 = (bf16[4,1,48,1280]{3,2,1,0:T(8,128)(2,1)}, bf16[4,1,48,1280]{3,2,1,0:T(8,128)(2,1)S(1)}, u32[]{:S(2)}, u32[]{:S(2)}) collective-permute-start(bf16[4,1,48,1280]{3,2,1,0:T(8,128)(2,1)} %get-tuple-element.202), channel_id=1, source_target_pairs={{0,4},{1,5},{2,6},{3,7},{4,0},{5,1},{6,2},{7,3},{8,12},{9,13},{10,... | collective-permute-start | bytes 1474568 | tf_op jit(solution)/shard_map/ppermute | solution.py:57
  241.7 14.3 %collective-permute-start.25 = (bf16[4,48,2048]{2,1,0:T(8,128)(2,1)}, bf16[4,48,2048]{2,1,0:T(8,128)(2,1)S(1)}, u32[]{:S(2)}, u32[]{:S(2)}) collective-permute-start(bf16[4,48,2048]{2,1,0:T(8,128)(2,1)} %get-tuple-element.200), channel_id=1, source_target_pairs={{0,1},{1,0},{2,6},{3,7},{4,5},{5,4},{6,2},{7,3},{8,9},{9,8},{10,14... | collective-permute-start | bytes 2359304 | tf_op jit(solution)/shard_map/ppermute | solution.py:57
  256.9 17.2 %collective-permute-start.29 = (bf16[48,2048]{1,0:T(8,128)(2,1)}, bf16[48,2048]{1,0:T(8,128)(2,1)S(1)}, u32[]{:S(2)}, u32[]{:S(2)}) collective-permute-start(bf16[48,2048]{1,0:T(8,128)(2,1)} %get-tuple-element.204), channel_id=1, source_target_pairs={{0,24},{1,25},{2,26},{3,27},{4,28},{5,29},{6,30},{7,31},{8,0},{9,1... | collective-permute-start | bytes 589832 | tf_op jit(solution)/shard_map/ppermute | solution.py:57
  258.8 17.2 %collective-permute-start.28 = (bf16[48,2048]{1,0:T(8,128)(2,1)S(1)}, bf16[48,2048]{1,0:T(8,128)(2,1)S(1)}, u32[]{:S(2)}, u32[]{:S(2)}) collective-permute-start(bf16[48,2048]{1,0:T(8,128)(2,1)S(1)} %get-tuple-element.205), channel_id=1, source_target_pairs={{0,16},{1,17},{2,18},{3,19},{4,20},{5,21},{6,22},{7,23},{8,24},{9,... | collective-permute-start | bytes 589832 | tf_op jit(solution)/shard_map/ppermute | solution.py:57
  259.9 16.0 %collective-permute-start.27 = (bf16[48,2048]{1,0:T(8,128)(2,1)S(1)}, bf16[48,2048]{1,0:T(8,128)(2,1)S(1)}, u32[]{:S(2)}, u32[]{:S(2)}) collective-permute-start(bf16[48,2048]{1,0:T(8,128)(2,1)S(1)} %get-tuple-element.206), channel_id=1, source_target_pairs={{0,8},{1,9},{2,10},{3,11},{4,12},{5,13},{6,14},{7,15},{8,16},{9,17... | collective-permute-start | bytes 589832 | tf_op jit(solution)/shard_map/ppermute | solution.py:57
  262.3 34.2 %collective-permute-start.32 = (bf16[4,1,48,1280]{3,2,1,0:T(8,128)(2,1)S(1)}, bf16[4,1,48,1280]{3,2,1,0:T(8,128)(2,1)}, u32[]{:S(2)}, u32[]{:S(2)}) collective-permute-start(bf16[4,1,48,1280]{3,2,1,0:T(8,128)(2,1)S(1)} %fusion.2), channel_id=1, source_target_pairs={{0,1},{1,0},{2,3},{3,2},{4,5},{5,4},{6,7},{7,6},{8,9},{9,8},{10,11... | collective-permute-start | bytes 1474568 | tf_op jit(solution)/shard_map/ppermute | solution.py:57
  297.7 16.0 %collective-permute-start.33 = (bf16[1,48,1280]{2,1,0:T(8,128)(2,1)S(1)}, bf16[1,48,1280]{2,1,0:T(8,128)(2,1)S(1)}, u32[]{:S(2)}, u32[]{:S(2)}) collective-permute-start(bf16[1,48,1280]{2,1,0:T(8,128)(2,1)S(1)} %get-tuple-element.208), channel_id=1, source_target_pairs={{0,8},{1,9},{2,10},{3,11},{4,12},{5,13},{6,14},{7,15},{8,16},{9,17... | collective-permute-start | bytes 368648 | tf_op jit(solution)/shard_map/ppermute | solution.py:57
  300.2 13.5 %collective-permute-start.34 = (bf16[1,48,1280]{2,1,0:T(8,128)(2,1)S(1)}, bf16[1,48,1280]{2,1,0:T(8,128)(2,1)S(1)}, u32[]{:S(2)}, u32[]{:S(2)}) collective-permute-start(bf16[1,48,1280]{2,1,0:T(8,128)(2,1)S(1)} %get-tuple-element.209), channel_id=1, source_target_pairs={{0,16},{1,17},{2,18},{3,19},{4,20},{5,21},{6,22},{7,23},{8,24},{9,... | collective-permute-start | bytes 368648 | tf_op jit(solution)/shard_map/ppermute | solution.py:57
  (30 other events, 277.9 us)
Sparse Core Ops, SparseCore 0:
  65.1 60.1 all-gather.4
  147.5 107.8 reduce-scatter.1
  257.0 53.3 all-gather.6
